TPU v7x, 32 devices: a whole 2x2x4 slice. The times are simulated.
32 devices in a mesh: grp: 2 (over core), batch: 16 (over z, y, x).
Axes of the slice: x: 2, y: 2, z: 4, core: 2. Of those that a mesh axis runs over, the one named last changes fastest.
Arguments:
- latent: bfloat16 [286720, 256], P(('grp', 'batch')), may hold values from -6 to 6
- future_latent: bfloat16 [286720, 256], P(('grp', 'batch')), may hold values from -6 to 6
- actions: int32 [286720], P(('grp', 'batch')), may hold values from 0 to 3
- codes: int32 [286720], P(('grp', 'batch')), may hold values from 0 to 31
- lengths: int32 [57344], P(('grp', 'batch')), may hold values from 1 to 5
- w_lat: bfloat16 [256, 256], replicated, may hold values from -0.375 to 0.375
- w_act: bfloat16 [4, 256], replicated, may hold values from -4 to 4
- gain_input: float32 [256], replicated, may hold values from 0.1 to 1.9
- gain_block: float32 [256], replicated, may hold values from 0.1 to 1.9
- w_one: bfloat16 [256, 256], replicated, may hold values from -0.375 to 0.375
- w_two: bfloat16 [256, 256], replicated, may hold values from -0.5 to 0.5
- gain_head: float32 [256], replicated, may hold values from 0.1 to 1.9
- w_chance: bfloat16 [256, 32], replicated, may hold values from -0.5 to 0.5
- w_value: bfloat16 [256, 601], replicated, may hold values from -0.5 to 0.5
- w_target: bfloat16 [256, 601], replicated, may hold values from -0.5 to 0.5
Outputs:
- grad_latent: float32 [286720, 256], P(('grp', 'batch'))
- grad_w_lat: float32 [256, 256], replicated
- grad_w_act: float32 [4, 256], replicated
- grad_gain_input: float32 [256], replicated
- grad_gain_block: float32 [256], replicated
- grad_w_one: float32 [256, 256], replicated
- grad_w_two: float32 [256, 256], replicated
- grad_gain_head: float32 [256], replicated
- grad_w_chance: float32 [256, 32], replicated
- grad_w_value: float32 [256, 601], replicated
All inputs are finite; a program needn't handle non-finite values.
Results may differ from a plain program's by a relative error of at most 0.007.
The roundings to bfloat16 on the way count: a program that leaves them out, or rounds other values in their place, can miss the bound.
Values may be sent and summed in bfloat16 or wider, within the bound.
No kernel may reach another device: no remote copies, remote signals or barrier semaphores. Data moves between devices by JAX's collectives and lax.ppermute only.
A program may use at most 256 MiB of HBM per device.

v0:
```python
import functools
import math

import jax
import jax.numpy as jnp
from jax import lax
from jax.experimental import pallas as pl
from jax.experimental.pallas import tpu as pltpu
from jax.sharding import PartitionSpec as P

D = 256
ACTIONS = 4
CODES = 32
BINS = 601
UNROLL = 5
EPSILON = 1e-05
WIDE = 640
CODE_AT = WIDE - CODES
ROWS = 1280
F32 = jnp.float32
BF16 = jnp.bfloat16

AT_HEAD = 0
AT_TWO = 640
AT_ONE = 896
AT_LAT = 1152
AT_ACT = 1408
AT_GAIN = 1424
PACKED = 1536


def dot(left, right, over_left, over_right):
    return lax.dot_general(
        left,
        right,
        (((over_left,), (over_right,)), ((), ())),
        preferred_element_type=F32,
    )


def norm_forward(value, gain):
    center = value - jnp.mean(value, axis=1, keepdims=True)
    scaled = lax.rsqrt(jnp.mean(center * center, axis=1, keepdims=True) + EPSILON)
    normed = center * scaled
    return normed * gain, normed, scaled


def norm_backward(grad, gain, normed, scaled):
    gained = grad * gain
    along = grad * normed
    gain_grad = jnp.sum(along.reshape(-1, 8, D), axis=0)
    centered = (
        gained
        - jnp.mean(gained, axis=1, keepdims=True)
        - normed * jnp.mean(along * gain, axis=1, keepdims=True)
    )
    return scaled * centered, gain_grad


def pieces(value):
    return [value[:, at : at + 128] for at in range(0, WIDE, 128)]


def exps_and_sum(logits):
    top = jnp.max(functools.reduce(jnp.maximum, logits), axis=1, keepdims=True)
    exps = [jnp.exp(piece - top) for piece in logits]
    return exps, jnp.sum(functools.reduce(jnp.add, exps), axis=1, keepdims=True)


def tower(scale, first, *refs):
    (latent_ref, moved_ref, index_ref, w_lat, w_act, gain_in, gain_bl, gain_he) = refs[:8]
    (w_one, w_two, w_chance, w_value, w_target) = refs[8:13]
    if first:
        grad_latent, packed, heads, encoder, acts, picks = refs[13:]
    else:
        before, _, grad_latent, packed, heads, encoder, acts, picks = refs[13:]
    rows = latent_ref.shape[0]

    @pl.when(pl.program_id(0) == 0)
    def _():
        gap = jnp.zeros((D, CODE_AT - BINS), F32)
        heads[...] = jnp.concatenate(
            [w_value[...].astype(F32), gap, w_chance[...].astype(F32)], axis=1
        ).astype(BF16)
        encoder[...] = jnp.concatenate(
            [w_target[...].astype(F32), jnp.zeros((D, WIDE - BINS), F32)], axis=1
        ).astype(BF16)
        acts[...] = jnp.concatenate(
            [w_act[...].astype(F32), jnp.zeros((16 - ACTIONS, D), F32)], axis=0
        ).astype(BF16)
        row = lax.broadcasted_iota(jnp.int32, (48, D), 0)
        col = lax.broadcasted_iota(jnp.int32, (48, D), 1)
        coded = (row < CODES) & (col == row + 128 - CODES)
        picks[...] = jnp.where(coded | ((row == CODES) & (col >= 128)), 1.0, 0.0).astype(BF16)
        packed[...] = jnp.zeros_like(packed) if first else before[...]

    lane = lax.broadcasted_iota(jnp.int32, (1, 128), 1)
    hide_value = jnp.where(lane < BINS - (WIDE - 128), 0.0, -1e30)
    hide_code = jnp.where(lane >= 128 - CODES, 0.0, -1e30)
    index = index_ref[...].reshape(3, rows)
    act_hot = (lax.broadcasted_iota(jnp.int32, (16, rows), 0) == index[0:1]).astype(F32)
    act_hot = act_hot.astype(BF16)
    kind = lax.broadcasted_iota(jnp.int32, (48, rows), 0)
    row_facts = jnp.where(
        kind == CODES, index[2:3].astype(F32), (kind == index[1:2]).astype(F32)
    ).astype(BF16)

    latent = latent_ref[...]
    pre = dot(latent, w_lat[...], 1, 0) + dot(act_hot, acts[...], 0, 0)
    first_out, first_norm, first_scale = norm_forward(pre, gain_in[...])
    state = jnp.maximum(first_out, 0.0)
    second_out, second_norm, second_scale = norm_forward(state, gain_bl[...])
    inner = jnp.maximum(second_out, 0.0).astype(BF16)
    hidden = jnp.maximum(dot(inner, w_one[...], 1, 0), 0.0).astype(BF16)
    out = state + dot(hidden, w_two[...], 1, 0)
    head_out, head_norm, head_scale = norm_forward(out, gain_he[...])
    head = head_out.astype(BF16)

    facts = dot(row_facts, picks[...], 0, 0)
    code_hot = facts[:, :128]
    weight = facts[:, 128:] * scale

    logits = pieces(dot(moved_ref[...], encoder[...], 1, 0))
    exps, total = exps_and_sum(logits[:4] + [logits[4] + hide_value])
    share = 1.0 / total
    target = [(e * share).astype(BF16).astype(F32) for e in exps]

    logits = pieces(dot(head, heads[...], 1, 0))
    exps, total = exps_and_sum(logits[:4] + [logits[4] + hide_value])
    share = 1.0 / total
    code_exps, code_total = exps_and_sum([logits[4] + hide_code])
    grads = [e * share - t for e, t in zip(exps, target)]
    grads[4] = grads[4] + (code_exps[0] * (1.0 / code_total) - code_hot)
    grad_logits = jnp.concatenate([(g * weight).astype(BF16) for g in grads], axis=1)

    grad_heads = dot(head, grad_logits, 0, 0)
    packed[0:256, :] += grad_heads[:, 0:256]
    packed[256:512, :] += grad_heads[:, 256:512]
    packed[512:640, 0:128] += grad_heads[0:128, 512:640]
    packed[512:640, 128:256] += grad_heads[128:256, 512:640]
    grad_head = dot(grad_logits, heads[...], 1, 1)

    grad_out, gain = norm_backward(grad_head, gain_he[...], head_norm, head_scale)
    packed[AT_GAIN + 16 : AT_GAIN + 24, :] += gain
    grad_branch = grad_out.astype(BF16)
    packed[AT_TWO : AT_TWO + 256, :] += dot(hidden, grad_branch, 0, 0)
    grad_zed = jnp.where(
        hidden > 0, dot(grad_branch, w_two[...], 1, 1).astype(BF16), jnp.zeros((), BF16)
    )
    packed[AT_ONE : AT_ONE + 256, :] += dot(inner, grad_zed, 0, 0)
    grad_second = jnp.where(second_out > 0, dot(grad_zed, w_one[...], 1, 1), 0.0)
    through, gain = norm_backward(grad_second, gain_bl[...], second_norm, second_scale)
    packed[AT_GAIN + 8 : AT_GAIN + 16, :] += gain
    grad_first = jnp.where(first_out > 0, grad_out + through, 0.0)
    grad_pre, gain = norm_backward(grad_first, gain_in[...], first_norm, first_scale)
    packed[AT_GAIN : AT_GAIN + 8, :] += gain
    grad_pre = grad_pre.astype(BF16)
    packed[AT_LAT : AT_LAT + 256, :] += dot(latent, grad_pre, 0, 0)
    packed[AT_ACT : AT_ACT + 16, :] += dot(act_hot, grad_pre, 1, 0)
    grad_latent[...] = dot(grad_pre, w_lat[...], 1, 1)


def run_tower(scale, at, steps, latent, moved, index, weights, before):
    rows = latent.shape[0]

    def whole(array):
        zeros = (0,) * array.ndim
        return pl.BlockSpec(array.shape, lambda i: zeros)

    def blocks(start):
        return pl.BlockSpec((ROWS, D), lambda i: (i + start, 0))

    first = before is None
    in_specs = [blocks(at), blocks(0), pl.BlockSpec((3, 1, ROWS), lambda i: (0, 0, i + at))]
    in_specs += [whole(w) for w in weights]
    args = [latent, moved, index, *weights]
    aliases = {}
    if not first:
        in_specs += [pl.BlockSpec((PACKED, D), lambda i: (0, 0)), pl.BlockSpec(memory_space=pl.ANY)]
        args += [before[1], before[0]]
        aliases = {len(args) - 1: 0}
    return pl.pallas_call(
        functools.partial(tower, scale, first),
        grid=(steps,),
        in_specs=in_specs,
        out_specs=[blocks(at), pl.BlockSpec((PACKED, D), lambda i: (0, 0))],
        out_shape=[
            jax.ShapeDtypeStruct((rows, D), F32),
            jax.ShapeDtypeStruct((PACKED, D), F32),
        ],
        scratch_shapes=[
            pltpu.VMEM((D, WIDE), BF16),
            pltpu.VMEM((D, WIDE), BF16),
            pltpu.VMEM((16, D), BF16),
            pltpu.VMEM((48, D), BF16),
        ],
        input_output_aliases=aliases,
        compiler_params=pltpu.CompilerParams(vmem_limit_bytes=60 << 20),
        cost_estimate=pl.CostEstimate(
            flops=steps * ROWS * 2500000,
            bytes_accessed=steps * ROWS * 2048,
            transcendentals=steps * ROWS * 1280,
        ),
        name="tower",
    )(*args)


def sum_over_all(packed):
    rows = packed.shape[0] // 2
    core = lax.axis_index("grp")
    count = lax.axis_size("batch")
    swap = [(0, 1), (1, 0)]
    low, high = packed[:rows], packed[rows:]
    keep = jnp.where(core == 0, low, high)
    other = jnp.where(core == 0, high, low)
    mine = keep + lax.ppermute(other, "grp", swap)
    share = lax.all_to_all(mine.reshape(count, -1, D), "batch", 0, 0, tiled=True)
    share = jnp.sum(share, axis=0)
    mine = jnp.broadcast_to(share[None], (count, *share.shape))
    mine = lax.all_to_all(mine, "batch", 0, 0, tiled=True).reshape(rows, D)
    other = lax.ppermute(mine, "grp", swap)
    low = jnp.where(core == 0, mine, other)
    high = jnp.where(core == 0, other, mine)
    return jnp.concatenate([low, high], axis=0)


def body(
    latent,
    future_latent,
    actions,
    codes,
    lengths,
    w_lat,
    w_act,
    gain_input,
    gain_block,
    w_one,
    w_two,
    gain_head,
    w_chance,
    w_value,
    w_target,
):
    rows = latent.shape[0]
    swap = [(0, 1), (1, 0)]
    moved_a = lax.ppermute(future_latent[:ROWS], "grp", swap)
    moved_b = lax.ppermute(future_latent[ROWS:], "grp", swap)
    traj_total = lengths.shape[0] * lax.axis_size("grp") * lax.axis_size("batch")
    steps_idx = jnp.arange(UNROLL, dtype=jnp.int32)
    mask = (steps_idx[None, :] < lengths[:, None]).astype(jnp.int32).reshape(-1)
    index = jnp.stack([actions, codes, mask])[:, None, :]
    weights = (
        w_lat,
        w_act,
        gain_input[None],
        gain_block[None],
        gain_head[None],
        w_one,
        w_two,
        w_chance,
        w_value,
        w_target,
    )
    scale = 1.0 / math.sqrt(traj_total)
    part = run_tower(scale, 0, 1, latent, moved_a, index, weights, None)
    grad_latent, packed = run_tower(
        scale, 1, rows // ROWS - 1, latent, moved_b, index, weights, part
    )
    packed = sum_over_all(packed)
    tail = packed[512:640].reshape(128, 2, 128).transpose(1, 0, 2).reshape(D, 128)
    grad_w_value = jnp.concatenate(
        [packed[0:256], packed[256:512], tail[:, : BINS - 512]], axis=1
    )
    gains = jnp.sum(packed[AT_GAIN : AT_GAIN + 24].reshape(3, 8, D), axis=1)
    return (
        grad_latent,
        packed[AT_LAT : AT_LAT + 256],
        packed[AT_ACT : AT_ACT + ACTIONS],
        gains[0],
        gains[1],
        packed[AT_ONE : AT_ONE + 256],
        packed[AT_TWO : AT_TWO + 256],
        gains[2],
        tail[:, 128 - CODES :],
        grad_w_value,
    )


def solution(mesh):
    split = P(("grp", "batch"))
    rows = P(("grp", "batch"), None)
    in_specs = (rows, rows, split, split, split) + (P(),) * 10
    out_specs = (rows,) + (P(),) * 9
    return jax.shard_map(body, mesh=mesh, in_specs=in_specs, out_specs=out_specs, check_vma=False)
```

profile of v0, /device:TPU:0, one launch (start us, length us, event | category | flops | bytes accessed | tf_op | source)
XLA Modules:
  0.0 143.1 jit_solution(14714198469569634707)
XLA Ops:
  0.6 0.0 copy-start.5
  0.7 0.0 copy-start.2
  0.7 0.0 copy-start.3
  0.7 0.0 copy-start
  0.7 4.3 %slice.51 = bf16[7680,256]{1,0:T(8,128)(2,1)} slice(bf16[8960,256]{1,0:T(8,128)(2,1)} %param.16), slice={[1280:8960], [0:256]} | slice | bytes 7864320 | tf_op jit(solution)/shard_map/slice | solution.py:247
  5.0 0.0 copy-start.1
  5.0 0.0 copy-start.4
  5.0 0.5 collective-permute-start
  5.5 1.1 slice.52
  6.6 0.1 collective-permute-start.1
  6.7 0.0 copy-done.5
  6.7 0.3 fusion
  7.1 0.6 reshape.69
  7.7 0.0 copy-done.2
  7.7 0.0 copy-done.3
  7.8 0.1 pad_add_fusion
  7.9 0.7 broadcast_in_dim.20.refs_2_
  8.6 0.0 copy-done
  8.6 0.9 copy.39.refs_11_
  9.5 0.0 copy-done.1
  9.5 0.9 copy.40.refs_12_
  10.4 0.0 copy-done.4
  10.4 0.7 copy.38.refs_10_
  11.1 1.9 %collective-permute-done.1.refs_1_ = bf16[1280,256]{1,0:T(8,128)(2,1)S(1)} collective-permute-done((bf16[1280,256]{1,0:T(8,128)(2,1)S(1)}, bf16[1280,256]{1,0:T(8,128)(2,1)S(1)}, u32[]{:S(2)}, u32[]{:S(2)}) %collective-permute-start.1) | collective-permute-done | bytes 655392 | tf_op jit(solution)/shard_map/ppermute | solution.py:246
  13.0 0.0 copy-start.6
  13.0 0.8 copy-done.6
  13.9 11.2 %tower.2 = (f32[8960,256]{1,0:T(8,128)}, f32[1536,256]{1,0:T(8,128)}) custom-call(bf16[8960,256]{1,0:T(8,128)(2,1)} %refs_0_.3, bf16[1280,256]{1,0:T(8,128)(2,1)} %copy-done.6, s32[3,1,8960]{2,1,0:T(1,128)} %broadcast_in_dim.20.refs_2_, bf16[256,256]{1,0:T(8,128)(2,1)} %refs_3_.3, bf16[4,256]{1,0:T(4,128)(2,1)} %refs_4_.3, f32[1,256]{1,0:T(1,128)} %bitcast.30, ...), custom_call_target="tpu_custom_call" | custom-call | flops 3200000000 | bytes 2621440 | tf_op jit(solution)/shard_map/tower/pallas_call | solution.py:182
  25.1 0.0 collective-permute-done.refs_1_
  25.1 52.6 %tower.3 = (f32[8960,256]{1,0:T(8,128)}, f32[1536,256]{1,0:T(8,128)}) custom-call(bf16[8960,256]{1,0:T(8,128)(2,1)} %refs_0_.3, bf16[7680,256]{1,0:T(8,128)(2,1)} %collective-permute-done.refs_1_, s32[3,1,8960]{2,1,0:T(1,128)} %broadcast_in_dim.20.refs_2_, bf16[256,256]{1,0:T(8,128)(2,1)} %refs_3_.3, ...), custom_call_target="tpu_custom_call", output_to_operand_aliasing={{0}: (14, {})} | custom-call | flops 19200000000 | bytes 15728640 | tf_op jit(solution)/shard_map/tower/pallas_call | solution.py:182
  77.7 1.5 %slice_select_fusion = f32[768,256]{1,0:T(8,128)S(1)} fusion(f32[1536,256]{1,0:T(8,128)} %get-tuple-element.17, pred[]{:T(512)S(6)} %eq.2), kind=kLoop, calls=%fused_computation.3 | loop fusion | flops 196608 | bytes 2359297 | tf_op jit(solution)/shard_map/jit(_where)/select_n | solution.py:215
  79.2 0.4 collective-permute-start.2
  79.6 1.9 %collective-permute-done.2 = f32[768,256]{1,0:T(8,128)S(1)} collective-permute-done((f32[768,256]{1,0:T(8,128)S(1)}, f32[768,256]{1,0:T(8,128)S(1)}, u32[]{:S(2)}, u32[]{:S(2)}) %collective-permute-start.2) | collective-permute-done | bytes 786464 | tf_op jit(solution)/shard_map/ppermute | solution.py:216
  81.5 1.5 %select_add_fusion = f32[768,256]{1,0:T(8,128)S(1)} fusion(f32[768,256]{1,0:T(8,128)S(1)} %collective-permute-done.2, f32[1536,256]{1,0:T(8,128)} %get-tuple-element.17, pred[]{:T(512)S(6)} %eq.2), kind=kLoop, calls=%fused_computation.2 | loop fusion | flops 393216 | bytes 3145729 | tf_op jit(solution)/shard_map/add | solution.py:216
  83.0 29.6 %all_to_all.10 = f32[16,48,256]{2,1,0:T(8,128)S(1)} all-to-all(f32[16,48,256]{2,1,0:T(8,128)S(1)} %bitcast.24), channel_id=1, replica_groups=mesh['grp'=2,'batch'=16] {'batch'}, dimensions={0} | all-to-all | bytes 1572864 | tf_op jit(solution)/shard_map/all_to_all | solution.py:217
  112.6 0.1 reduce_sum.18
  112.7 0.1 broadcast_in_dim.24
  112.8 23.9 %all_to_all.11 = f32[16,48,256]{2,1,0:T(8,128)S(1)} all-to-all(f32[16,48,256]{2,1,0:T(8,128)S(1)} %broadcast_in_dim.24), channel_id=1, replica_groups=mesh['grp'=2,'batch'=16] {'batch'}, dimensions={0} | all-to-all | bytes 1572864 | tf_op jit(solution)/shard_map/all_to_all | solution.py:220
  136.7 0.0 collective-permute-start.3
  136.7 2.3 %collective-permute-done.3 = f32[768,256]{1,0:T(8,128)S(1)} collective-permute-done((f32[768,256]{1,0:T(8,128)S(1)}, f32[768,256]{1,0:T(8,128)S(1)}, u32[]{:S(2)}, u32[]{:S(2)}) %collective-permute-start.3) | collective-permute-done | bytes 786464 | tf_op jit(solution)/shard_map/ppermute | solution.py:221
  139.0 0.1 broadcast_select_fusion
  139.1 0.9 fusion.2
  140.0 0.6 slice.69
  140.6 0.1 slice.76
  140.8 1.1 copy.43
  141.8 0.7 copy.42
  142.5 0.6 fusion.3
  (5 shorter events, 0.1 us)
Async XLA Ops:
  0.6 6.1 %copy-start.5 = (s32[1792]{0:T(1024)S(1)}, s32[1792]{0:T(1024)}, u32[]{:S(2)}) copy-start(s32[1792]{0:T(1024)} %param.19) | copy-start | bytes 21508
  0.7 7.0 %copy-start.2 = (s32[8960]{0:T(1024)S(1)}, s32[8960]{0:T(1024)}, u32[]{:S(2)}) copy-start(s32[8960]{0:T(1024)} %param.18) | copy-start | bytes 107524
  0.7 7.1 %copy-start.3 = (s32[8960]{0:T(1024)S(1)}, s32[8960]{0:T(1024)}, u32[]{:S(2)}) copy-start(s32[8960]{0:T(1024)} %param.17) | copy-start | bytes 107524
  0.7 7.9 %copy-start = (bf16[256,601]{0,1:T(8,128)(2,1)S(1)}, bf16[256,601]{0,1:T(8,128)(2,1)}, u32[]{:S(2)}) copy-start(bf16[256,601]{0,1:T(8,128)(2,1)} %param.28) | copy-start | bytes 923140
  5.0 4.5 %copy-start.1 = (bf16[256,601]{0,1:T(8,128)(2,1)S(1)}, bf16[256,601]{0,1:T(8,128)(2,1)}, u32[]{:S(2)}) copy-start(bf16[256,601]{0,1:T(8,128)(2,1)} %param.29) | copy-start | bytes 923140
  5.0 5.4 %copy-start.4 = (bf16[256,32]{0,1:T(8,128)(2,1)S(1)}, bf16[256,32]{0,1:T(8,128)(2,1)}, u32[]{:S(2)}) copy-start(bf16[256,32]{0,1:T(8,128)(2,1)} %param.27) | copy-start | bytes 49156
  5.0 20.1 %collective-permute-start = (bf16[7680,256]{1,0:T(8,128)(2,1)}, bf16[7680,256]{1,0:T(8,128)(2,1)}, u32[]{:S(2)}, u32[]{:S(2)}) collective-permute-start(bf16[7680,256]{1,0:T(8,128)(2,1)} %slice.51), channel_id=1, source_target_pairs={{0,16},{16,0},{1,17},{17,1},{2,18},{18,2},{3,19},{19,3},{4,20},{20... | collective-permute-start | bytes 11796488 | tf_op jit(solution)/shard_map/ppermute | solution.py:247
  6.6 6.4 %collective-permute-start.1 = (bf16[1280,256]{1,0:T(8,128)(2,1)S(1)}, bf16[1280,256]{1,0:T(8,128)(2,1)S(1)}, u32[]{:S(2)}, u32[]{:S(2)}) collective-permute-start(bf16[1280,256]{1,0:T(8,128)(2,1)S(1)} %slice.52), channel_id=1, source_target_pairs={{0,16},{16,0},{1,17},{17,1},{2,18},{18,2},{3,19},{19,3},{4,20},{20... | collective-permute-start | bytes 1966088 | tf_op jit(solution)/shard_map/ppermute | solution.py:246
  13.0 0.8 copy-start.6
  79.2 2.4 %collective-permute-start.2 = (f32[768,256]{1,0:T(8,128)S(1)}, f32[768,256]{1,0:T(8,128)S(1)}, u32[]{:S(2)}, u32[]{:S(2)}) collective-permute-start(f32[768,256]{1,0:T(8,128)S(1)} %slice_select_fusion), channel_id=1, source_target_pairs={{0,16},{16,0},{1,17},{17,1},{2,18},{18,2},{3,19},{19,3},{4,20},{20... | collective-permute-start | bytes 2359304 | tf_op jit(solution)/shard_map/ppermute | solution.py:216
  136.7 2.3 %collective-permute-start.3 = (f32[768,256]{1,0:T(8,128)S(1)}, f32[768,256]{1,0:T(8,128)S(1)}, u32[]{:S(2)}, u32[]{:S(2)}) collective-permute-start(f32[768,256]{1,0:T(8,128)S(1)} %bitcast.23), channel_id=1, source_target_pairs={{0,16},{16,0},{1,17},{17,1},{2,18},{18,2},{3,19},{19,3},{4,20},{20... | collective-permute-start | bytes 2359304 | tf_op jit(solution)/shard_map/ppermute | solution.py:221
where the time goes:
time: 143 us
  Pallas kernels  63.8 us (45%)
  blocking collectives  53.5 us (37%)
  local copies, waits for them, and re-layouts  13.3 us (9%)
  waiting for transfers between devices  6.12 us (4%)
  other arithmetic  4.51 us (3%)
    pallas_call x2, Pallas kernels, run_tower(): pl.pallas_call(functools.partial(tower, scale, first), grid=(steps,), in_...  63.8 us
    all_to_all x1, blocking collectives, sum_over_all(): lax.all_to_all(mine.reshape(count, -1, D), 'batch', 0, 0, tiled=True)  29.6 us
    all_to_all x1, blocking collectives, sum_over_all(): mine = lax.all_to_all(mine, 'batch', 0, 0, tiled=True).reshape(rows, D)  23.9 us
    unnamed x19, local copies, waits for them, and re-layouts  5.14 us
    slice x1, local copies, waits for them, and re-layouts, body(): moved_b = lax.ppermute(future_latent[ROWS:], 'grp', swap)  4.31 us
  transfers between devices with their start and end apart: 4, of which 3 were waited for; matrix products, arithmetic and copies ran while one was open for 4% of the time, Pallas kernels for 8%

commit v1 on v0

v1 whole, which is shorter than its diff:
```python
import functools
import math

import jax
import jax.numpy as jnp
from jax import lax
from jax.experimental import pallas as pl
from jax.experimental.pallas import tpu as pltpu
from jax.sharding import PartitionSpec as P

D = 256
ACTIONS = 4
CODES = 32
BINS = 601
UNROLL = 5
EPSILON = 1e-05
WIDE = 640
CODE_AT = WIDE - CODES
ROWS = 1280
F32 = jnp.float32
BF16 = jnp.bfloat16

AT_TWO = 640
AT_ONE = 896
AT_LAT = 1152
AT_ACT = 1408
AT_GAIN = 1424
PACKED = 1536
HALF = PACKED // 2
RUN_TWO = 0
RUN_ONE = 256
RUN_LAT = 512
RUN_ACT = 768
RUN_GAIN = 784
RUNNING = 808


def dot(left, right, over_left, over_right):
    return lax.dot_general(
        left,
        right,
        (((over_left,), (over_right,)), ((), ())),
        preferred_element_type=F32,
    )


def norm_forward(value, gain):
    center = value - jnp.mean(value, axis=1, keepdims=True)
    scaled = lax.rsqrt(jnp.mean(center * center, axis=1, keepdims=True) + EPSILON)
    normed = center * scaled
    return normed * gain, normed, scaled


def norm_backward(grad, gain, normed, scaled):
    gained = grad * gain
    along = grad * normed
    gain_grad = jnp.sum(along.reshape(-1, 8, D), axis=0)
    centered = (
        gained
        - jnp.mean(gained, axis=1, keepdims=True)
        - normed * jnp.mean(along * gain, axis=1, keepdims=True)
    )
    return scaled * centered, gain_grad


def pieces(value):
    return [value[:, at : at + 128] for at in range(0, WIDE, 128)]


def exps_and_sum(logits):
    top = jnp.max(functools.reduce(jnp.maximum, logits), axis=1, keepdims=True)
    exps = [jnp.exp(piece - top) for piece in logits]
    return exps, jnp.sum(functools.reduce(jnp.add, exps), axis=1, keepdims=True)


def tower(scale, first, *refs):
    (core, latent_ref, moved_ref, index_ref, w_lat, w_act, gain_in, gain_bl, gain_he) = refs[:9]
    (w_one, w_two, w_chance, w_value, w_target) = refs[9:14]
    if first:
        grad_latent, head_sums, sums, heads, encoder, acts, picks = refs[14:]
    else:
        head_before, before, _, grad_latent, stay, send = refs[14:20]
        heads, encoder, acts, picks, head_sums, sums, packed = refs[20:]
    rows = latent_ref.shape[0]

    @pl.when(pl.program_id(0) == 0)
    def _():
        gap = jnp.zeros((CODE_AT - BINS, D), F32)
        heads[...] = jnp.concatenate(
            [w_value[...].astype(F32), gap, w_chance[...].astype(F32)], axis=0
        ).astype(BF16)
        encoder[...] = jnp.concatenate(
            [w_target[...].astype(F32), jnp.zeros((WIDE - BINS, D), F32)], axis=0
        ).astype(BF16)
        acts[...] = jnp.concatenate(
            [w_act[...].astype(F32), jnp.zeros((16 - ACTIONS, D), F32)], axis=0
        ).astype(BF16)
        row = lax.broadcasted_iota(jnp.int32, (48, D), 0)
        col = lax.broadcasted_iota(jnp.int32, (48, D), 1)
        coded = (row < CODES) & (col == row + 128 - CODES)
        picks[...] = jnp.where(coded | ((row == CODES) & (col >= 128)), 1.0, 0.0).astype(BF16)
        head_sums[...] = jnp.zeros_like(head_sums) if first else head_before[...]
        sums[...] = jnp.zeros_like(sums) if first else before[...]

    lane = lax.broadcasted_iota(jnp.int32, (1, 128), 1)
    hide_value = jnp.where(lane < BINS - (WIDE - 128), 0.0, -1e30)
    hide_code = jnp.where(lane >= 128 - CODES, 0.0, -1e30)
    index = index_ref[...].reshape(3, rows)
    act_hot = (lax.broadcasted_iota(jnp.int32, (16, rows), 0) == index[0:1]).astype(F32)
    act_hot = act_hot.astype(BF16)
    kind = lax.broadcasted_iota(jnp.int32, (48, rows), 0)
    row_facts = jnp.where(
        kind == CODES, index[2:3].astype(F32), (kind == index[1:2]).astype(F32)
    ).astype(BF16)

    latent = latent_ref[...]
    pre = dot(latent, w_lat[...], 1, 0) + dot(act_hot, acts[...], 0, 0)
    first_out, first_norm, first_scale = norm_forward(pre, gain_in[...])
    state = jnp.maximum(first_out, 0.0)
    second_out, second_norm, second_scale = norm_forward(state, gain_bl[...])
    inner = jnp.maximum(second_out, 0.0).astype(BF16)
    hidden = jnp.maximum(dot(inner, w_one[...], 1, 0), 0.0).astype(BF16)
    out = state + dot(hidden, w_two[...], 1, 0)
    head_out, head_norm, head_scale = norm_forward(out, gain_he[...])
    head = head_out.astype(BF16)

    facts = dot(row_facts, picks[...], 0, 0)
    code_hot = facts[:, :128]
    weight = facts[:, 128:] * scale

    logits = pieces(dot(moved_ref[...], encoder[...], 1, 1))
    exps, total = exps_and_sum(logits[:4] + [logits[4] + hide_value])
    share = 1.0 / total
    target = [(e * share).astype(BF16).astype(F32) for e in exps]

    logits = pieces(dot(head, heads[...], 1, 1))
    exps, total = exps_and_sum(logits[:4] + [logits[4] + hide_value])
    share = 1.0 / total
    code_exps, code_total = exps_and_sum([logits[4] + hide_code])
    grads = [e * share - t for e, t in zip(exps, target)]
    grads[4] = grads[4] + (code_exps[0] * (1.0 / code_total) - code_hot)
    grad_logits = jnp.concatenate([(g * weight).astype(BF16) for g in grads], axis=1)

    head_sums[...] += dot(head, grad_logits, 0, 0)
    grad_head = dot(grad_logits, heads[...], 1, 0)

    grad_out, gain = norm_backward(grad_head, gain_he[...], head_norm, head_scale)
    sums[RUN_GAIN + 16 : RUN_GAIN + 24, :] += gain
    grad_branch = grad_out.astype(BF16)
    sums[RUN_TWO : RUN_TWO + 256, :] += dot(hidden, grad_branch, 0, 0)
    grad_zed = jnp.where(
        hidden > 0, dot(grad_branch, w_two[...], 1, 1).astype(BF16), jnp.zeros((), BF16)
    )
    sums[RUN_ONE : RUN_ONE + 256, :] += dot(inner, grad_zed, 0, 0)
    grad_second = jnp.where(second_out > 0, dot(grad_zed, w_one[...], 1, 1), 0.0)
    through, gain = norm_backward(grad_second, gain_bl[...], second_norm, second_scale)
    sums[RUN_GAIN + 8 : RUN_GAIN + 16, :] += gain
    grad_first = jnp.where(first_out > 0, grad_out + through, 0.0)
    grad_pre, gain = norm_backward(grad_first, gain_in[...], first_norm, first_scale)
    sums[RUN_GAIN : RUN_GAIN + 8, :] += gain
    grad_pre = grad_pre.astype(BF16)
    sums[RUN_LAT : RUN_LAT + 256, :] += dot(latent, grad_pre, 0, 0)
    sums[RUN_ACT : RUN_ACT + 16, :] += dot(act_hot, grad_pre, 1, 0)
    grad_latent[...] = dot(grad_pre, w_lat[...], 1, 1)


    if not first:

        @pl.when(pl.program_id(0) == pl.num_programs(0) - 1)
        def _():
            packed[0:WIDE, :] = head_sums[...].T
            packed[AT_TWO:AT_GAIN, :] = sums[0:RUN_GAIN, :]
            gains = [
                jnp.sum(sums[RUN_GAIN + at : RUN_GAIN + at + 8, :], axis=0, keepdims=True)
                for at in (0, 8, 16)
            ]
            gains.append(jnp.zeros((PACKED - AT_GAIN - 3, D), F32))
            packed[AT_GAIN:, :] = jnp.concatenate(gains, axis=0)
            mine = pl.multiple_of(core[0] * HALF, HALF)
            stay[...] = packed[pl.ds(mine, HALF), :]
            send[...] = packed[pl.ds(HALF - mine, HALF), :].astype(BF16)


def unpack(core, mine, other, lat, act, gain_in, gain_bl, one, two, gain_he, chance, value, packed):
    at = pl.multiple_of(core[0] * HALF, HALF)
    packed[pl.ds(at, HALF), :] = mine[...].astype(F32)
    packed[pl.ds(HALF - at, HALF), :] = other[...].astype(F32)
    value[...] = packed[0:BINS, :]
    chance[...] = packed[CODE_AT:WIDE, :]
    two[...] = packed[AT_TWO : AT_TWO + D, :]
    one[...] = packed[AT_ONE : AT_ONE + D, :]
    lat[...] = packed[AT_LAT : AT_LAT + D, :]
    act[...] = packed[AT_ACT : AT_ACT + ACTIONS, :]
    gain_in[...] = packed[AT_GAIN : AT_GAIN + 1, :]
    gain_bl[...] = packed[AT_GAIN + 1 : AT_GAIN + 2, :]
    gain_he[...] = packed[AT_GAIN + 2 : AT_GAIN + 3, :]


def run_tower(scale, core, at, steps, latent, moved, index, weights, before):
    rows = latent.shape[0]

    def whole(array):
        zeros = (0,) * array.ndim
        return pl.BlockSpec(array.shape, lambda i: zeros)

    def shape(rows, cols, kind=F32):
        return jax.ShapeDtypeStruct((rows, cols), kind)

    blocks = pl.BlockSpec((ROWS, D), lambda i: (i + at, 0))
    first = before is None
    in_specs = [pl.BlockSpec(memory_space=pltpu.SMEM), blocks, blocks]
    in_specs += [pl.BlockSpec((3, 1, ROWS), lambda i: (0, 0, i + at))]
    in_specs += [whole(w) for w in weights]
    args = [core, latent, moved, index, *weights]
    scratch = [
        pltpu.VMEM((WIDE, D), BF16),
        pltpu.VMEM((WIDE, D), BF16),
        pltpu.VMEM((16, D), BF16),
        pltpu.VMEM((48, D), BF16),
    ]
    aliases = {}
    if first:
        results = [shape(D, WIDE), shape(RUNNING, D)]
    else:
        results = [shape(HALF, D), shape(HALF, D, BF16)]
        scratch += [pltpu.VMEM((D, WIDE), F32), pltpu.VMEM((RUNNING, D), F32)]
        scratch += [pltpu.VMEM((PACKED, D), F32)]
        in_specs += [whole(before[1]), whole(before[2]), pl.BlockSpec(memory_space=pl.ANY)]
        args += [before[1], before[2], before[0]]
        aliases = {len(args) - 1: 0}
    return pl.pallas_call(
        functools.partial(tower, scale, first),
        grid=(steps,),
        in_specs=in_specs,
        out_specs=[blocks] + [whole(r) for r in results],
        out_shape=[shape(rows, D)] + results,
        scratch_shapes=scratch,
        input_output_aliases=aliases,
        compiler_params=pltpu.CompilerParams(vmem_limit_bytes=60 << 20),
        cost_estimate=pl.CostEstimate(
            flops=steps * ROWS * 2500000,
            bytes_accessed=steps * ROWS * 2048,
            transcendentals=steps * ROWS * 1280,
        ),
        name="tower",
    )(*args)


def sum_over_chips(mine):
    count = lax.axis_size("batch")
    near = 8 if count == 16 else count
    groups = [[at * near + i for i in range(near)] for at in range(count // near)]
    swap = functools.partial(
        lax.all_to_all,
        axis_name="batch",
        split_axis=0,
        concat_axis=0,
        tiled=True,
        axis_index_groups=groups,
    )
    rows = mine.shape[0]
    share = swap(mine.reshape(near, -1, D))
    share = jnp.sum(share.astype(F32), axis=0).astype(BF16)
    if count == 2 * near:
        far = lax.ppermute(share, "batch", [(i, (i + near) % count) for i in range(count)])
        share = (share.astype(F32) + far.astype(F32)).astype(BF16)
    return swap(jnp.broadcast_to(share[None], (near, *share.shape))).reshape(rows, D)


def finish(core, stay, send):
    swap = [(0, 1), (1, 0)]
    mine = (stay + lax.ppermute(send, "grp", swap).astype(F32)).astype(BF16)
    mine = sum_over_chips(mine)
    other = lax.ppermute(mine, "grp", swap)
    sizes = (D, ACTIONS, 1, 1, D, D, 1, CODES, BINS)
    return pl.pallas_call(
        unpack,
        in_specs=[pl.BlockSpec(memory_space=pltpu.SMEM)] + [pl.BlockSpec(memory_space=pltpu.VMEM)] * 2,
        out_shape=[jax.ShapeDtypeStruct((n, D), F32) for n in sizes],
        scratch_shapes=[pltpu.VMEM((PACKED, D), F32)],
        name="unpack",
    )(core, mine, other)


def body(
    latent,
    future_latent,
    actions,
    codes,
    lengths,
    w_lat,
    w_act,
    gain_input,
    gain_block,
    w_one,
    w_two,
    gain_head,
    w_chance,
    w_value,
    w_target,
):
    rows = latent.shape[0]
    swap = [(0, 1), (1, 0)]
    moved_a = lax.ppermute(future_latent[:ROWS], "grp", swap)
    moved_b = lax.ppermute(future_latent, "grp", swap)
    traj_total = lengths.shape[0] * lax.axis_size("grp") * lax.axis_size("batch")
    steps_idx = jnp.arange(UNROLL, dtype=jnp.int32)
    mask = (steps_idx[None, :] < lengths[:, None]).astype(jnp.int32).reshape(-1)
    index = jnp.stack([actions, codes, mask])[:, None, :]
    weights = (
        w_lat,
        w_act,
        gain_input[None],
        gain_block[None],
        gain_head[None],
        w_one,
        w_two,
        w_chance.T,
        w_value.T,
        w_target.T,
    )
    scale = 1.0 / math.sqrt(traj_total)
    core = lax.axis_index("grp").astype(jnp.int32).reshape(1)
    part = run_tower(scale, core, 0, 1, latent, moved_a, index, weights, None)
    grad_latent, stay, send = run_tower(
        scale, core, 1, rows // ROWS - 1, latent, moved_b, index, weights, part
    )
    lat, act, gain_in, gain_bl, one, two, gain_he, chance, value = finish(core, stay, send)
    return (
        grad_latent,
        lat,
        act,
        gain_in[0],
        gain_bl[0],
        one,
        two,
        gain_he[0],
        chance.T,
        value.T,
    )


def solution(mesh):
    split = P(("grp", "batch"))
    rows = P(("grp", "batch"), None)
    in_specs = (rows, rows, split, split, split) + (P(),) * 10
    out_specs = (rows,) + (P(),) * 9
    return jax.shard_map(body, mesh=mesh, in_specs=in_specs, out_specs=out_specs, check_vma=False)
```

time: 143 us -> 113 us (0.79)
  blocking collectives: 53.5 us -> 24.3 us
  local copies, waits for them, and re-layouts: 13.3 us -> 5.7 us
  waiting for transfers between devices: 6.12 us -> 9.44 us
  starting transfers between devices: 1.05 us -> 3.73 us
  Pallas kernels: 63.8 us -> 66.3 us
  other arithmetic: 4.51 us -> 2.38 us
    all_to_all x2, blocking collectives: 53.5 us -> 24.3 us  [the longest x1 14.4 us: sum_over_chips(): share = swap(mine.reshape(near, -1, D))]
    slice x4 -> x0, local copies, waits for them, and re-layouts: 5.56 us -> none  [the longest x1 4.31 us: body(): moved_b = lax.ppermute(future_latent[ROWS:], 'grp', swap)]
    unnamed x19 -> x6, local copies, waits for them, and re-layouts: 5.14 us -> 1.61 us
    ppermute x3 -> x4, starting transfers between devices: 0.93 us -> 3.65 us  [the longest x1 2.65 us: sum_over_chips(): lax.ppermute(share, 'batch', [(i, (i + near) % count) for i in range(coun...]
    pallas_call x0 -> x1, Pallas kernels: none -> 2.33 us  [finish(): pl.pallas_call(unpack, in_specs=[pl.BlockSpec(memory_space=pltpu.SMEM)] +...]
    ppermute x3 -> x4, waiting for transfers between devices: 4.2 us -> 6.21 us  [the longest x1 2.93 us: sum_over_chips(): lax.ppermute(share, 'batch', [(i, (i + near) % count) for i in range(coun...]
    select_n x2 -> x0, other arithmetic: 1.58 us -> none  [the longest x1 1.47 us: sum_over_all(): other = jnp.where(core == 0, high, low)]
    another operation x2, local copies, waits for them, and re-layouts: 0.05 us -> 1.59 us  [body(): index = jnp.stack([actions, codes, mask])[:, None, :]]
  transfers between devices with their start and end apart: 4 -> 5, of which waited for: 3 -> 4; matrix products, arithmetic and copies ran while one was open for 4% -> 5% of each run, Pallas kernels for 8% -> 10%
where the time goes in v1:
time: 113 us; the launch traced here: 112 us
  Pallas kernels  66.3 us (59%)
  blocking collectives  24.3 us (22%)
  waiting for transfers between devices  9.44 us (8%)
  local copies, waits for them, and re-layouts  5.7 us (5%)
  starting transfers between devices  3.73 us (3%)
  other arithmetic  2.38 us (2%)
    pallas_call x2, Pallas kernels, run_tower(): pl.pallas_call(functools.partial(tower, scale, first), grid=(steps,), in_...  63.9 us
    all_to_all x1, blocking collectives, sum_over_chips(): share = swap(mine.reshape(near, -1, D))  14.4 us
    all_to_all x1, blocking collectives, sum_over_chips(): swap(jnp.broadcast_to(share[None], (near, *share.shape))).reshape(rows, D)  9.89 us
    ppermute x1, waiting for transfers between devices, body(): moved_a = lax.ppermute(future_latent[:ROWS], 'grp', swap)  3.23 us
    ppermute x1, waiting for transfers between devices, sum_over_chips(): lax.ppermute(share, 'batch', [(i, (i + near) % count) for i in range(coun...  2.93 us
    ppermute x1, starting transfers between devices, sum_over_chips(): lax.ppermute(share, 'batch', [(i, (i + near) % count) for i in range(coun...  2.65 us
    pallas_call x1, Pallas kernels, finish(): pl.pallas_call(unpack, in_specs=[pl.BlockSpec(memory_space=pltpu.SMEM)] +...  2.33 us
  transfers between devices with their start and end apart: 5, of which 4 were waited for; matrix products, arithmetic and copies ran while one was open for 5% of the time, Pallas kernels for 10%

profile of v1, /device:TPU:0, one launch (start us, length us, event | category | flops | bytes accessed | tf_op | source)
XLA Modules:
  0.0 112.5 jit_solution(14329282788285050530)
XLA Ops:
  0.6 0.6 collective-permute-start
  1.2 1.1 %slice.3 = bf16[1280,256]{1,0:T(8,128)(2,1)S(1)} slice(bf16[8960,256]{1,0:T(8,128)(2,1)} %param.16), slice={[0:1280], [0:256]} | slice | bytes 1310720 | tf_op jit(solution)/shard_map/slice | solution.py:304
  2.3 0.1 collective-permute-start.1
  2.4 0.8 stack.9
  3.2 0.8 stack.10
  4.0 1.0 fusion
  5.0 0.6 reshape.61
  5.6 0.1 pad_add_fusion
  5.7 0.7 broadcast_in_dim.20.refs_3_
  6.5 3.2 %collective-permute-done.1.refs_2_ = bf16[1280,256]{1,0:T(8,128)(2,1)S(1)} collective-permute-done((bf16[1280,256]{1,0:T(8,128)(2,1)S(1)}, bf16[1280,256]{1,0:T(8,128)(2,1)S(1)}, u32[]{:S(2)}, u32[]{:S(2)}) %collective-permute-start.1) | collective-permute-done | bytes 655392 | tf_op jit(solution)/shard_map/ppermute | solution.py:304
  9.7 0.0 copy-start.2
  9.7 0.9 copy-done.2
  10.6 10.9 %tower.2 = (f32[8960,256]{1,0:T(8,128)}, f32[256,640]{1,0:T(8,128)}, f32[808,256]{1,0:T(8,128)}) custom-call(s32[1]{0:T(128)} %bitcast.refs_0_.core, bf16[8960,256]{1,0:T(8,128)(2,1)} %refs_1_.3, bf16[1280,256]{1,0:T(8,128)(2,1)} %copy-done.2, s32[3,1,8960]{2,1,0:T(1,128)} %broadcast_in_dim.20.refs_3_, bf16[256,256]{1,0:T(8,128)(2,1)} %refs_4_.3, ...), custom_call_target="tpu_custom_call" | custom-call | flops 3200000000 | bytes 2621440 | tf_op jit(solution)/shard_map/tower/pallas_call | solution.py:231
  21.4 0.0 collective-permute-done.refs_2_
  21.4 53.0 %tower.3 = (f32[8960,256]{1,0:T(8,128)}, f32[768,256]{1,0:T(8,128)}, bf16[768,256]{1,0:T(8,128)(2,1)}) custom-call(s32[1]{0:T(128)} %bitcast.refs_0_.core, bf16[8960,256]{1,0:T(8,128)(2,1)} %refs_1_.3, bf16[8960,256]{1,0:T(8,128)(2,1)} %collective-permute-done.refs_2_, s32[3,1,8960]{2,1,0:T(1,128)} %broadcast_in_dim.20.refs_3_, ...), custom_call_target="tpu_custom_call", output_to_operand_aliasing={{0}: (16, {})} | custom-call | flops 19200000000 | bytes 15728640 | tf_op jit(solution)/shard_map/tower/pallas_call | solution.py:231
  74.5 0.4 collective-permute-start.2
  74.9 1.6 %collective-permute-done.2 = bf16[768,256]{1,0:T(8,128)(2,1)S(1)} collective-permute-done((bf16[768,256]{1,0:T(8,128)(2,1)}, bf16[768,256]{1,0:T(8,128)(2,1)S(1)}, u32[]{:S(2)}, u32[]{:S(2)}) %collective-permute-start.2) | collective-permute-done | bytes 393248 | tf_op jit(solution)/shard_map/ppermute | solution.py:272
  76.5 1.2 %add_convert_fusion = bf16[768,256]{1,0:T(8,128)(2,1)S(1)} fusion(f32[768,256]{1,0:T(8,128)} %get-tuple-element.29, bf16[768,256]{1,0:T(8,128)(2,1)S(1)} %collective-permute-done.2), kind=kLoop, calls=%fused_computation.2 | loop fusion | flops 589824 | bytes 1572864 | tf_op jit(solution)/shard_map/convert_element_type | solution.py:272
  77.7 14.4 %all_to_all.10 = bf16[8,96,256]{2,1,0:T(8,128)(2,1)S(1)} all-to-all(bf16[8,96,256]{2,1,0:T(8,128)(2,1)S(1)} %bitcast.16), channel_id=1, replica_groups={{0,1,2,3,4,5,6,7},{8,9,10,11,12,13,14,15},{16,17,18,19,20,21,22,23},{24..., dimensions={0} | all-to-all | bytes 786432 | tf_op jit(solution)/shard_map/all_to_all | solution.py:262
  92.1 0.1 reduce_sum.12
  92.1 2.7 %collective-permute-start.3 = (bf16[96,256]{1,0:T(8,128)(2,1)S(1)}, bf16[96,256]{1,0:T(8,128)(2,1)S(1)}, u32[]{:S(2)}, u32[]{:S(2)}) collective-permute-start(bf16[96,256]{1,0:T(8,128)(2,1)S(1)} %reduce_sum.12), channel_id=1, source_target_pairs={{0,8},{1,9},{2,10},{3,11},{4,12},{5,13},{6,14},{7,15},{8,0},{9,1},... | collective-permute-start | bytes 147464 | tf_op jit(solution)/shard_map/ppermute | solution.py:265
  94.8 2.9 %collective-permute-done.3 = bf16[96,256]{1,0:T(8,128)(2,1)S(1)} collective-permute-done((bf16[96,256]{1,0:T(8,128)(2,1)S(1)}, bf16[96,256]{1,0:T(8,128)(2,1)S(1)}, u32[]{:S(2)}, u32[]{:S(2)}) %collective-permute-start.3) | collective-permute-done | bytes 49184 | tf_op jit(solution)/shard_map/ppermute | solution.py:265
  97.8 9.9 %all_to_all.11 = bf16[8,96,256]{2,1,0:T(8,128)(2,1)S(1)} all-to-all(bf16[8,96,256]{2,1,0:T(8,128)(2,1)S(1)} %broadcast_in_dim.24), channel_id=1, replica_groups={{0,1,2,3,4,5,6,7},{8,9,10,11,12,13,14,15},{16,17,18,19,20,21,22,23},{24..., dimensions={0} | all-to-all | bytes 786432 | tf_op jit(solution)/shard_map/all_to_all | solution.py:267
  107.7 0.0 copy-start
  107.7 0.0 collective-permute-start.4
  107.7 1.7 %collective-permute-done.4.other = bf16[768,256]{1,0:T(8,128)(2,1)S(1)} collective-permute-done((bf16[768,256]{1,0:T(8,128)(2,1)S(1)}, bf16[768,256]{1,0:T(8,128)(2,1)S(1)}, u32[]{:S(2)}, u32[]{:S(2)}) %collective-permute-start.4) | collective-permute-done | bytes 393248 | tf_op jit(solution)/shard_map/ppermute | solution.py:274
  109.4 0.0 copy-done
  109.4 0.0 copy-start.1
  109.4 0.8 copy-done.1
  110.2 2.3 %unpack.1 = (f32[256,256]{1,0:T(8,128)}, f32[4,256]{1,0:T(4,128)}, f32[1,256]{1,0:T(1,128)}, f32[1,256]{1,0:T(1,128)}, f32[256,256]{1,0:T(8,128)}, /*index=5*/f3...) custom-call(s32[1]{0:T(128)} %bitcast.refs_0_.core, bf16[768,256]{1,0:T(8,128)(2,1)} %bitcast.15, ...), custom_call_target="tpu_custom_call" | custom-call | tf_op jit(solution)/shard_map/unpack/pallas_call | solution.py:276
  (2 shorter events, 0.0 us)
Async XLA Ops:
  0.6 20.8 %collective-permute-start = (bf16[8960,256]{1,0:T(8,128)(2,1)}, bf16[8960,256]{1,0:T(8,128)(2,1)}, u32[]{:S(2)}, u32[]{:S(2)}) collective-permute-start(bf16[8960,256]{1,0:T(8,128)(2,1)} %param.16), channel_id=1, source_target_pairs={{0,16},{16,0},{1,17},{17,1},{2,18},{18,2},{3,19},{19,3},{4,20},{20... | collective-permute-start | bytes 13762568 | tf_op jit(solution)/shard_map/ppermute | solution.py:305
  2.3 7.4 %collective-permute-start.1 = (bf16[1280,256]{1,0:T(8,128)(2,1)S(1)}, bf16[1280,256]{1,0:T(8,128)(2,1)S(1)}, u32[]{:S(2)}, u32[]{:S(2)}) collective-permute-start(bf16[1280,256]{1,0:T(8,128)(2,1)S(1)} %slice.3), channel_id=1, source_target_pairs={{0,16},{16,0},{1,17},{17,1},{2,18},{18,2},{3,19},{19,3},{4,20},{20... | collective-permute-start | bytes 1966088 | tf_op jit(solution)/shard_map/ppermute | solution.py:304
  9.7 0.9 copy-start.2
  74.5 2.0 %collective-permute-start.2 = (bf16[768,256]{1,0:T(8,128)(2,1)}, bf16[768,256]{1,0:T(8,128)(2,1)S(1)}, u32[]{:S(2)}, u32[]{:S(2)}) collective-permute-start(bf16[768,256]{1,0:T(8,128)(2,1)} %get-tuple-element.30), channel_id=1, source_target_pairs={{0,16},{16,0},{1,17},{17,1},{2,18},{18,2},{3,19},{19,3},{4,20},{20... | collective-permute-start | bytes 1179656 | tf_op jit(solution)/shard_map/ppermute | solution.py:272
  92.1 5.6 %collective-permute-start.3 = (bf16[96,256]{1,0:T(8,128)(2,1)S(1)}, bf16[96,256]{1,0:T(8,128)(2,1)S(1)}, u32[]{:S(2)}, u32[]{:S(2)}) collective-permute-start(bf16[96,256]{1,0:T(8,128)(2,1)S(1)} %reduce_sum.12), channel_id=1, source_target_pairs={{0,8},{1,9},{2,10},{3,11},{4,12},{5,13},{6,14},{7,15},{8,0},{9,1},... | collective-permute-start | bytes 147464 | tf_op jit(solution)/shard_map/ppermute | solution.py:265
  107.7 1.7 %copy-start = (bf16[8,96,256]{2,1,0:T(8,128)(2,1)}, bf16[8,96,256]{2,1,0:T(8,128)(2,1)S(1)}, u32[]{:S(2)}) copy-start(bf16[8,96,256]{2,1,0:T(8,128)(2,1)S(1)} %all_to_all.11) | copy-start | bytes 1179652
  107.7 1.7 %collective-permute-start.4 = (bf16[768,256]{1,0:T(8,128)(2,1)S(1)}, bf16[768,256]{1,0:T(8,128)(2,1)S(1)}, u32[]{:S(2)}, u32[]{:S(2)}) collective-permute-start(bf16[768,256]{1,0:T(8,128)(2,1)S(1)} %bitcast.14), channel_id=1, source_target_pairs={{0,16},{16,0},{1,17},{17,1},{2,18},{18,2},{3,19},{19,3},{4,20},{20... | collective-permute-start | bytes 1179656 | tf_op jit(solution)/shard_map/ppermute | solution.py:274
  109.4 0.8 copy-start.1

commit v2 on v1

--- a/solution.py
+++ b/solution.py
@@ -17,6 +17,8 @@
 WIDE = 640
 CODE_AT = WIDE - CODES
 ROWS = 1280
+SUB = 640
+LAG = 6
 F32 = jnp.float32
 BF16 = jnp.bfloat16
 
@@ -44,23 +46,25 @@
     )
 
 
-def norm_forward(value, gain):
+def normalize(value):
     center = value - jnp.mean(value, axis=1, keepdims=True)
     scaled = lax.rsqrt(jnp.mean(center * center, axis=1, keepdims=True) + EPSILON)
-    normed = center * scaled
-    return normed * gain, normed, scaled
+    return center * scaled, scaled
 
 
 def norm_backward(grad, gain, normed, scaled):
     gained = grad * gain
-    along = grad * normed
-    gain_grad = jnp.sum(along.reshape(-1, 8, D), axis=0)
+    along = gained * normed
     centered = (
         gained
         - jnp.mean(gained, axis=1, keepdims=True)
-        - normed * jnp.mean(along * gain, axis=1, keepdims=True)
-    )
-    return scaled * centered, gain_grad
+        - normed * jnp.mean(along, axis=1, keepdims=True)
+    )
+    return scaled * centered, jnp.sum(along.reshape(-1, 8, D), axis=0)
+
+
+def add_up(parts):
+    return jnp.sum(parts.reshape(-1, 8, D), axis=0)
 
 
 def pieces(value):
@@ -105,64 +109,114 @@
     lane = lax.broadcasted_iota(jnp.int32, (1, 128), 1)
     hide_value = jnp.where(lane < BINS - (WIDE - 128), 0.0, -1e30)
     hide_code = jnp.where(lane >= 128 - CODES, 0.0, -1e30)
-    index = index_ref[...].reshape(3, rows)
-    act_hot = (lax.broadcasted_iota(jnp.int32, (16, rows), 0) == index[0:1]).astype(F32)
-    act_hot = act_hot.astype(BF16)
-    kind = lax.broadcasted_iota(jnp.int32, (48, rows), 0)
-    row_facts = jnp.where(
-        kind == CODES, index[2:3].astype(F32), (kind == index[1:2]).astype(F32)
-    ).astype(BF16)
-
-    latent = latent_ref[...]
-    pre = dot(latent, w_lat[...], 1, 0) + dot(act_hot, acts[...], 0, 0)
-    first_out, first_norm, first_scale = norm_forward(pre, gain_in[...])
-    state = jnp.maximum(first_out, 0.0)
-    second_out, second_norm, second_scale = norm_forward(state, gain_bl[...])
-    inner = jnp.maximum(second_out, 0.0).astype(BF16)
-    hidden = jnp.maximum(dot(inner, w_one[...], 1, 0), 0.0).astype(BF16)
-    out = state + dot(hidden, w_two[...], 1, 0)
-    head_out, head_norm, head_scale = norm_forward(out, gain_he[...])
-    head = head_out.astype(BF16)
-
-    facts = dot(row_facts, picks[...], 0, 0)
-    code_hot = facts[:, :128]
-    weight = facts[:, 128:] * scale
-
-    logits = pieces(dot(moved_ref[...], encoder[...], 1, 1))
-    exps, total = exps_and_sum(logits[:4] + [logits[4] + hide_value])
-    share = 1.0 / total
-    target = [(e * share).astype(BF16).astype(F32) for e in exps]
-
-    logits = pieces(dot(head, heads[...], 1, 1))
-    exps, total = exps_and_sum(logits[:4] + [logits[4] + hide_value])
-    share = 1.0 / total
-    code_exps, code_total = exps_and_sum([logits[4] + hide_code])
-    grads = [e * share - t for e, t in zip(exps, target)]
-    grads[4] = grads[4] + (code_exps[0] * (1.0 / code_total) - code_hot)
-    grad_logits = jnp.concatenate([(g * weight).astype(BF16) for g in grads], axis=1)
-
-    head_sums[...] += dot(head, grad_logits, 0, 0)
-    grad_head = dot(grad_logits, heads[...], 1, 0)
-
-    grad_out, gain = norm_backward(grad_head, gain_he[...], head_norm, head_scale)
-    sums[RUN_GAIN + 16 : RUN_GAIN + 24, :] += gain
-    grad_branch = grad_out.astype(BF16)
-    sums[RUN_TWO : RUN_TWO + 256, :] += dot(hidden, grad_branch, 0, 0)
-    grad_zed = jnp.where(
-        hidden > 0, dot(grad_branch, w_two[...], 1, 1).astype(BF16), jnp.zeros((), BF16)
-    )
-    sums[RUN_ONE : RUN_ONE + 256, :] += dot(inner, grad_zed, 0, 0)
-    grad_second = jnp.where(second_out > 0, dot(grad_zed, w_one[...], 1, 1), 0.0)
-    through, gain = norm_backward(grad_second, gain_bl[...], second_norm, second_scale)
-    sums[RUN_GAIN + 8 : RUN_GAIN + 16, :] += gain
-    grad_first = jnp.where(first_out > 0, grad_out + through, 0.0)
-    grad_pre, gain = norm_backward(grad_first, gain_in[...], first_norm, first_scale)
-    sums[RUN_GAIN : RUN_GAIN + 8, :] += gain
-    grad_pre = grad_pre.astype(BF16)
-    sums[RUN_LAT : RUN_LAT + 256, :] += dot(latent, grad_pre, 0, 0)
-    sums[RUN_ACT : RUN_ACT + 16, :] += dot(act_hot, grad_pre, 1, 0)
-    grad_latent[...] = dot(grad_pre, w_lat[...], 1, 1)
-
+
+    def one_part(at):
+        span = slice(at, at + SUB)
+        index = index_ref[:, :, span].reshape(3, SUB)
+        act_hot = (lax.broadcasted_iota(jnp.int32, (16, SUB), 0) == index[0:1]).astype(F32)
+        act_hot = act_hot.astype(BF16)
+        kind = lax.broadcasted_iota(jnp.int32, (48, SUB), 0)
+        row_facts = jnp.where(
+            kind == CODES, index[2:3].astype(F32), (kind == index[1:2]).astype(F32)
+        ).astype(BF16)
+
+        latent = latent_ref[span, :]
+        def first_norm_step(pre):
+            normed, scaled = normalize(pre)
+            return normed, scaled, jnp.maximum(normed * gain_in[...], 0.0)
+
+        def second_norm_step(state):
+            normed, scaled = normalize(state)
+            return normed, scaled, jnp.maximum(normed * gain_bl[...], 0.0).astype(BF16)
+
+        def head_norm_step(state, branch):
+            normed, scaled = normalize(state + branch)
+            return normed, scaled, (normed * gain_he[...]).astype(BF16)
+
+        def target_step(logits):
+            logits = pieces(logits)
+            exps, total = exps_and_sum(logits[:4] + [logits[4] + hide_value])
+            share = 1.0 / total
+            return (jnp.concatenate([(e * share).astype(BF16) for e in exps], axis=1),)
+
+        def loss_step(logits, target, facts):
+            code_hot = facts[:, :128]
+            weight = facts[:, 128:] * scale
+            target = [t.astype(F32) for t in pieces(target)]
+            logits = pieces(logits)
+            exps, total = exps_and_sum(logits[:4] + [logits[4] + hide_value])
+            share = 1.0 / total
+            code_exps, code_total = exps_and_sum([logits[4] + hide_code])
+            grads = [e * share - t for e, t in zip(exps, target)]
+            grads[4] = grads[4] + (code_exps[0] * (1.0 / code_total) - code_hot)
+            return (jnp.concatenate([(g * weight).astype(BF16) for g in grads], axis=1),)
+
+        def head_back_step(grad, normed, scaled):
+            grad, along = norm_backward(grad, gain_he[...], normed, scaled)
+            return grad, grad.astype(BF16), along
+
+        def zed_back_step(grad, hidden):
+            return (jnp.where(hidden > 0, grad.astype(BF16), jnp.zeros((), BF16)),)
+
+        def block_back_step(grad, normed, scaled, state, grad_out):
+            grad = jnp.where(normed > 0, grad, 0.0)
+            through, along = norm_backward(grad, gain_bl[...], normed, scaled)
+            return jnp.where(state > 0, grad_out + through, 0.0), along
+
+        def first_back_step(grad, normed, scaled):
+            grad, along = norm_backward(grad, gain_in[...], normed, scaled)
+            return grad.astype(BF16), along
+
+        pre = dot(latent, w_lat[...], 1, 0) + dot(act_hot, acts[...], 0, 0)
+        yield
+        first_norm, first_scale, state = first_norm_step(pre)
+        yield
+        second_norm, second_scale, inner = second_norm_step(state)
+        yield
+        hidden = jnp.maximum(dot(inner, w_one[...], 1, 0), 0.0).astype(BF16)
+        yield
+        branch = dot(hidden, w_two[...], 1, 0)
+        yield
+        head_norm, head_scale, head = head_norm_step(state, branch)
+        yield
+        logits = dot(moved_ref[span, :], encoder[...], 1, 1)
+        yield
+        (target,) = target_step(logits)
+        yield
+        facts = dot(row_facts, picks[...], 0, 0)
+        logits = dot(head, heads[...], 1, 1)
+        yield
+        (grad_logits,) = loss_step(logits, target, facts)
+        yield
+        grad_head = dot(grad_logits, heads[...], 1, 0)
+        head_sums[...] += dot(head, grad_logits, 0, 0)
+        yield
+        grad_out, grad_branch, along = head_back_step(grad_head, head_norm, head_scale)
+        sums[RUN_GAIN + 16 : RUN_GAIN + 24, :] += add_up(along)
+        yield
+        (grad_zed,) = zed_back_step(dot(grad_branch, w_two[...], 1, 1), hidden)
+        sums[RUN_TWO : RUN_TWO + 256, :] += dot(hidden, grad_branch, 0, 0)
+        yield
+        grad_inner = dot(grad_zed, w_one[...], 1, 1)
+        sums[RUN_ONE : RUN_ONE + 256, :] += dot(inner, grad_zed, 0, 0)
+        yield
+        grad_first, along = block_back_step(grad_inner, second_norm, second_scale, state, grad_out)
+        sums[RUN_GAIN + 8 : RUN_GAIN + 16, :] += add_up(along)
+        yield
+        grad_pre, along = first_back_step(grad_first, first_norm, first_scale)
+        sums[RUN_GAIN : RUN_GAIN + 8, :] += add_up(along)
+        yield
+        grad_latent[span, :] = dot(grad_pre, w_lat[...], 1, 1)
+        sums[RUN_LAT : RUN_LAT + 256, :] += dot(latent, grad_pre, 0, 0)
+        sums[RUN_ACT : RUN_ACT + 16, :] += dot(act_hot, grad_pre, 1, 0)
+
+    parts = [one_part(at) for at in range(0, rows, SUB)]
+    turn = 0
+    while any(parts):
+        for at, part in enumerate(parts):
+            if part and turn >= LAG * at and next(part, "end") == "end":
+                parts[at] = None
+        turn += 1
 
     if not first:
 
@@ -171,8 +225,8 @@
             packed[0:WIDE, :] = head_sums[...].T
             packed[AT_TWO:AT_GAIN, :] = sums[0:RUN_GAIN, :]
             gains = [
-                jnp.sum(sums[RUN_GAIN + at : RUN_GAIN + at + 8, :], axis=0, keepdims=True)
-                for at in (0, 8, 16)
+                jnp.sum(sums[RUN_GAIN + at : RUN_GAIN + at + 8, :], axis=0, keepdims=True) / gain[...]
+                for at, gain in ((0, gain_in), (8, gain_bl), (16, gain_he))
             ]
             gains.append(jnp.zeros((PACKED - AT_GAIN - 3, D), F32))
             packed[AT_GAIN:, :] = jnp.concatenate(gains, axis=0)
@@ -302,11 +356,12 @@
     rows = latent.shape[0]
     swap = [(0, 1), (1, 0)]
     moved_a = lax.ppermute(future_latent[:ROWS], "grp", swap)
-    moved_b = lax.ppermute(future_latent, "grp", swap)
     traj_total = lengths.shape[0] * lax.axis_size("grp") * lax.axis_size("batch")
     steps_idx = jnp.arange(UNROLL, dtype=jnp.int32)
     mask = (steps_idx[None, :] < lengths[:, None]).astype(jnp.int32).reshape(-1)
     index = jnp.stack([actions, codes, mask])[:, None, :]
+    moved_a, index, future_latent = lax.optimization_barrier((moved_a, index, future_latent))
+    moved_b = lax.ppermute(future_latent, "grp", swap)
     weights = (
         w_lat,
         w_act,

time: 113 us -> 105 us (0.929)
  Pallas kernels: 66.3 us -> 61.3 us
  waiting for transfers between devices: 9.44 us -> 6.58 us
    pallas_call x2, Pallas kernels: 63.9 us -> 59 us  [run_tower(): pl.pallas_call(functools.partial(tower, scale, first), grid=(steps,), in_...]
    ppermute x1, waiting for transfers between devices: 3.23 us -> 0.01 us  [body(): moved_a = lax.ppermute(future_latent[:ROWS], 'grp', swap)]
  transfers between devices with their start and end apart: 5 -> 5, of which waited for: 4 -> 3; matrix products, arithmetic and copies ran while one was open for 5% -> 4% of each run, Pallas kernels for 10% -> 10%
where the time goes in v2:
time: 105 us; the launch traced here: 104 us
  Pallas kernels  61.3 us (58%)
  blocking collectives  24.3 us (23%)
  waiting for transfers between devices  6.58 us (6%)
  local copies, waits for them, and re-layouts  5.68 us (5%)
  starting transfers between devices  3.3 us (3%)
  other arithmetic  2.38 us (2%)
    pallas_call x2, Pallas kernels, run_tower(): pl.pallas_call(functools.partial(tower, scale, first), grid=(steps,), in_...  59 us
    all_to_all x1, blocking collectives, sum_over_chips(): share = swap(mine.reshape(near, -1, D))  14.4 us
    all_to_all x1, blocking collectives, sum_over_chips(): swap(jnp.broadcast_to(share[None], (near, *share.shape))).reshape(rows, D)  9.89 us
    ppermute x1, waiting for transfers between devices, sum_over_chips(): lax.ppermute(share, 'batch', [(i, (i + near) % count) for i in range(coun...  2.93 us
    ppermute x1, starting transfers between devices, sum_over_chips(): lax.ppermute(share, 'batch', [(i, (i + near) % count) for i in range(coun...  2.65 us
    pallas_call x1, Pallas kernels, finish(): pl.pallas_call(unpack, in_specs=[pl.BlockSpec(memory_space=pltpu.SMEM)] +...  2.33 us
  transfers between devices with their start and end apart: 5, of which 3 were waited for; matrix products, arithmetic and copies ran while one was open for 4% of the time, Pallas kernels for 10%

profile of v2, /device:TPU:0, one launch (start us, length us, event | category | flops | bytes accessed | tf_op | source)
XLA Modules:
  0.0 104.2 jit_solution(7004495544561667376)
XLA Ops:
  0.6 1.1 %slice.3 = bf16[1280,256]{1,0:T(8,128)(2,1)S(1)} slice(bf16[8960,256]{1,0:T(8,128)(2,1)} %param.16), slice={[0:1280], [0:256]} | slice | bytes 1310720 | tf_op jit(solution)/shard_map/slice | solution.py:358
  1.8 0.6 collective-permute-start
  2.3 0.8 stack.9
  3.1 0.8 stack.10
  3.9 1.0 fusion
  4.9 0.6 reshape.61
  5.6 0.1 pad_add_fusion
  5.7 0.7 broadcast_in_dim.20.refs_3_
  6.4 0.0 collective-permute-done.refs_2_
  6.4 0.0 copy-start.2
  6.4 0.0 collective-permute-start.1
  6.4 0.8 copy-done.2
  7.2 10.2 %tower.2 = (f32[8960,256]{1,0:T(8,128)}, f32[256,640]{1,0:T(8,128)}, f32[808,256]{1,0:T(8,128)}) custom-call(s32[1]{0:T(128)} %bitcast.refs_0_.core, bf16[8960,256]{1,0:T(8,128)(2,1)} %refs_1_.3, bf16[1280,256]{1,0:T(8,128)(2,1)} %copy-done.2, s32[3,1,8960]{2,1,0:T(1,128)} %broadcast_in_dim.20.refs_3_, bf16[256,256]{1,0:T(8,128)(2,1)} %refs_4_.3, ...), custom_call_target="tpu_custom_call" | custom-call | flops 3200000000 | bytes 2621440 | tf_op jit(solution)/shard_map/tower/pallas_call | solution.py:285
  17.5 0.0 collective-permute-done.1.refs_2_
  17.5 48.7 %tower.3 = (f32[8960,256]{1,0:T(8,128)}, f32[768,256]{1,0:T(8,128)}, bf16[768,256]{1,0:T(8,128)(2,1)}) custom-call(s32[1]{0:T(128)} %bitcast.refs_0_.core, bf16[8960,256]{1,0:T(8,128)(2,1)} %refs_1_.3, bf16[8960,256]{1,0:T(8,128)(2,1)} %collective-permute-done.1.refs_2_, s32[3,1,8960]{2,1,0:T(1,128)} %broadcast_in_dim.20.refs_3_, ...), custom_call_target="tpu_custom_call", output_to_operand_aliasing={{0}: (16, {})} | custom-call | flops 19200000000 | bytes 15728640 | tf_op jit(solution)/shard_map/tower/pallas_call | solution.py:285
  66.2 0.1 collective-permute-start.2
  66.3 1.9 %collective-permute-done.2 = bf16[768,256]{1,0:T(8,128)(2,1)S(1)} collective-permute-done((bf16[768,256]{1,0:T(8,128)(2,1)}, bf16[768,256]{1,0:T(8,128)(2,1)S(1)}, u32[]{:S(2)}, u32[]{:S(2)}) %collective-permute-start.2) | collective-permute-done | bytes 393248 | tf_op jit(solution)/shard_map/ppermute | solution.py:326
  68.2 1.2 %add_convert_fusion = bf16[768,256]{1,0:T(8,128)(2,1)S(1)} fusion(f32[768,256]{1,0:T(8,128)} %get-tuple-element.35, bf16[768,256]{1,0:T(8,128)(2,1)S(1)} %collective-permute-done.2), kind=kLoop, calls=%fused_computation.2 | loop fusion | flops 589824 | bytes 1572864 | tf_op jit(solution)/shard_map/convert_element_type | solution.py:326
  69.4 14.4 %all_to_all.10 = bf16[8,96,256]{2,1,0:T(8,128)(2,1)S(1)} all-to-all(bf16[8,96,256]{2,1,0:T(8,128)(2,1)S(1)} %bitcast.16), channel_id=1, replica_groups={{0,1,2,3,4,5,6,7},{8,9,10,11,12,13,14,15},{16,17,18,19,20,21,22,23},{24..., dimensions={0} | all-to-all | bytes 786432 | tf_op jit(solution)/shard_map/all_to_all | solution.py:316
  83.8 0.1 reduce_sum.12
  83.9 2.6 %collective-permute-start.3 = (bf16[96,256]{1,0:T(8,128)(2,1)S(1)}, bf16[96,256]{1,0:T(8,128)(2,1)S(1)}, u32[]{:S(2)}, u32[]{:S(2)}) collective-permute-start(bf16[96,256]{1,0:T(8,128)(2,1)S(1)} %reduce_sum.12), channel_id=1, source_target_pairs={{0,8},{1,9},{2,10},{3,11},{4,12},{5,13},{6,14},{7,15},{8,0},{9,1},... | collective-permute-start | bytes 147464 | tf_op jit(solution)/shard_map/ppermute | solution.py:319
  86.5 2.9 %collective-permute-done.3 = bf16[96,256]{1,0:T(8,128)(2,1)S(1)} collective-permute-done((bf16[96,256]{1,0:T(8,128)(2,1)S(1)}, bf16[96,256]{1,0:T(8,128)(2,1)S(1)}, u32[]{:S(2)}, u32[]{:S(2)}) %collective-permute-start.3) | collective-permute-done | bytes 49184 | tf_op jit(solution)/shard_map/ppermute | solution.py:319
  89.5 9.9 %all_to_all.11 = bf16[8,96,256]{2,1,0:T(8,128)(2,1)S(1)} all-to-all(bf16[8,96,256]{2,1,0:T(8,128)(2,1)S(1)} %broadcast_in_dim.24), channel_id=1, replica_groups={{0,1,2,3,4,5,6,7},{8,9,10,11,12,13,14,15},{16,17,18,19,20,21,22,23},{24..., dimensions={0} | all-to-all | bytes 786432 | tf_op jit(solution)/shard_map/all_to_all | solution.py:321
  99.4 0.0 copy-start
  99.4 0.0 collective-permute-start.4
  99.4 1.7 %collective-permute-done.4.other = bf16[768,256]{1,0:T(8,128)(2,1)S(1)} collective-permute-done((bf16[768,256]{1,0:T(8,128)(2,1)S(1)}, bf16[768,256]{1,0:T(8,128)(2,1)S(1)}, u32[]{:S(2)}, u32[]{:S(2)}) %collective-permute-start.4) | collective-permute-done | bytes 393248 | tf_op jit(solution)/shard_map/ppermute | solution.py:328
  101.1 0.0 copy-done
  101.1 0.0 copy-start.1
  101.1 0.8 copy-done.1
  101.9 2.3 %unpack.1 = (f32[256,256]{1,0:T(8,128)}, f32[4,256]{1,0:T(4,128)}, f32[1,256]{1,0:T(1,128)}, f32[1,256]{1,0:T(1,128)}, f32[256,256]{1,0:T(8,128)}, /*index=5*/f3...) custom-call(s32[1]{0:T(128)} %bitcast.refs_0_.core, bf16[768,256]{1,0:T(8,128)(2,1)} %bitcast.15, ...), custom_call_target="tpu_custom_call" | custom-call | tf_op jit(solution)/shard_map/unpack/pallas_call | solution.py:330
  (2 shorter events, 0.0 us)
Async XLA Ops:
  1.8 4.6 %collective-permute-start = (bf16[1280,256]{1,0:T(8,128)(2,1)S(1)}, bf16[1280,256]{1,0:T(8,128)(2,1)S(1)}, u32[]{:S(2)}, u32[]{:S(2)}) collective-permute-start(bf16[1280,256]{1,0:T(8,128)(2,1)S(1)} %slice.3), channel_id=1, source_target_pairs={{0,16},{16,0},{1,17},{17,1},{2,18},{18,2},{3,19},{19,3},{4,20},{20... | collective-permute-start | bytes 1966088 | tf_op jit(solution)/shard_map/ppermute | solution.py:358
  6.4 0.9 copy-start.2
  6.4 11.1 %collective-permute-start.1 = (bf16[8960,256]{1,0:T(8,128)(2,1)}, bf16[8960,256]{1,0:T(8,128)(2,1)}, u32[]{:S(2)}, u32[]{:S(2)}) collective-permute-start(bf16[8960,256]{1,0:T(8,128)(2,1)} %param.16), channel_id=1, source_target_pairs={{0,16},{16,0},{1,17},{17,1},{2,18},{18,2},{3,19},{19,3},{4,20},{20... | collective-permute-start | bytes 13762568 | tf_op jit(solution)/shard_map/ppermute | solution.py:364
  66.2 2.0 %collective-permute-start.2 = (bf16[768,256]{1,0:T(8,128)(2,1)}, bf16[768,256]{1,0:T(8,128)(2,1)S(1)}, u32[]{:S(2)}, u32[]{:S(2)}) collective-permute-start(bf16[768,256]{1,0:T(8,128)(2,1)} %get-tuple-element.36), channel_id=1, source_target_pairs={{0,16},{16,0},{1,17},{17,1},{2,18},{18,2},{3,19},{19,3},{4,20},{20... | collective-permute-start | bytes 1179656 | tf_op jit(solution)/shard_map/ppermute | solution.py:326
  83.9 5.6 %collective-permute-start.3 = (bf16[96,256]{1,0:T(8,128)(2,1)S(1)}, bf16[96,256]{1,0:T(8,128)(2,1)S(1)}, u32[]{:S(2)}, u32[]{:S(2)}) collective-permute-start(bf16[96,256]{1,0:T(8,128)(2,1)S(1)} %reduce_sum.12), channel_id=1, source_target_pairs={{0,8},{1,9},{2,10},{3,11},{4,12},{5,13},{6,14},{7,15},{8,0},{9,1},... | collective-permute-start | bytes 147464 | tf_op jit(solution)/shard_map/ppermute | solution.py:319
  99.4 1.7 %copy-start = (bf16[8,96,256]{2,1,0:T(8,128)(2,1)}, bf16[8,96,256]{2,1,0:T(8,128)(2,1)S(1)}, u32[]{:S(2)}) copy-start(bf16[8,96,256]{2,1,0:T(8,128)(2,1)S(1)} %all_to_all.11) | copy-start | bytes 1179652
  99.4 1.7 %collective-permute-start.4 = (bf16[768,256]{1,0:T(8,128)(2,1)S(1)}, bf16[768,256]{1,0:T(8,128)(2,1)S(1)}, u32[]{:S(2)}, u32[]{:S(2)}) collective-permute-start(bf16[768,256]{1,0:T(8,128)(2,1)S(1)} %bitcast.14), channel_id=1, source_target_pairs={{0,16},{16,0},{1,17},{17,1},{2,18},{18,2},{3,19},{19,3},{4,20},{20... | collective-permute-start | bytes 1179656 | tf_op jit(solution)/shard_map/ppermute | solution.py:328
  101.1 0.8 copy-start.1

commit v3 on v2

--- a/solution.py
+++ b/solution.py
@@ -19,6 +19,25 @@
 ROWS = 1280
 SUB = 640
 LAG = 6
+STAGES = (
+    ("tl",),
+    ("pre",),
+    ("ln1",),
+    ("ln2",),
+    ("hid",),
+    ("branch",),
+    ("lnh",),
+    ("tsm",),
+    ("lg",),
+    ("lsm",),
+    ("gh", "hs"),
+    ("lbh",),
+    ("zed", "two"),
+    ("inn", "one"),
+    ("lbb",),
+    ("lbf",),
+    ("lat", "lats"),
+)
 F32 = jnp.float32
 BF16 = jnp.bfloat16
 
@@ -78,13 +97,13 @@
 
 
 def tower(scale, first, *refs):
-    (core, latent_ref, moved_ref, index_ref, w_lat, w_act, gain_in, gain_bl, gain_he) = refs[:9]
-    (w_one, w_two, w_chance, w_value, w_target) = refs[9:14]
+    (core, latent_ref, moved_ref, action_ref, code_ref, mask_ref) = refs[:6]
+    (w_lat, w_act, gain_in, gain_bl, gain_he, w_one, w_two, w_chance, w_value, w_target) = refs[6:16]
     if first:
-        grad_latent, head_sums, sums, heads, encoder, acts, picks = refs[14:]
+        grad_latent, head_sums, sums, heads, encoder, acts, picks = refs[16:]
     else:
-        head_before, before, _, grad_latent, stay, send = refs[14:20]
-        heads, encoder, acts, picks, head_sums, sums, packed = refs[20:]
+        head_before, before, _, grad_latent, stay, send = refs[16:22]
+        heads, encoder, acts, picks, head_sums, sums, packed = refs[22:]
     rows = latent_ref.shape[0]
 
     @pl.when(pl.program_id(0) == 0)
@@ -110,14 +129,19 @@
     hide_value = jnp.where(lane < BINS - (WIDE - 128), 0.0, -1e30)
     hide_code = jnp.where(lane >= 128 - CODES, 0.0, -1e30)
 
+    def target_step(logits):
+        logits = pieces(logits)
+        exps, total = exps_and_sum(logits[:4] + [logits[4] + hide_value])
+        share = 1.0 / total
+        return (jnp.concatenate([(e * share).astype(BF16) for e in exps], axis=1),)
+
     def one_part(at):
         span = slice(at, at + SUB)
-        index = index_ref[:, :, span].reshape(3, SUB)
-        act_hot = (lax.broadcasted_iota(jnp.int32, (16, SUB), 0) == index[0:1]).astype(F32)
-        act_hot = act_hot.astype(BF16)
+        act_hot = lax.broadcasted_iota(jnp.int32, (16, SUB), 0) == action_ref[:, span]
+        act_hot = act_hot.astype(F32).astype(BF16)
         kind = lax.broadcasted_iota(jnp.int32, (48, SUB), 0)
         row_facts = jnp.where(
-            kind == CODES, index[2:3].astype(F32), (kind == index[1:2]).astype(F32)
+            kind == CODES, mask_ref[:, span].astype(F32), (kind == code_ref[:, span]).astype(F32)
         ).astype(BF16)
 
         latent = latent_ref[span, :]
@@ -132,12 +156,6 @@
         def head_norm_step(state, branch):
             normed, scaled = normalize(state + branch)
             return normed, scaled, (normed * gain_he[...]).astype(BF16)
-
-        def target_step(logits):
-            logits = pieces(logits)
-            exps, total = exps_and_sum(logits[:4] + [logits[4] + hide_value])
-            share = 1.0 / total
-            return (jnp.concatenate([(e * share).astype(BF16) for e in exps], axis=1),)
 
         def loss_step(logits, target, facts):
             code_hot = facts[:, :128]
@@ -168,55 +186,62 @@
             return grad.astype(BF16), along
 
         pre = dot(latent, w_lat[...], 1, 0) + dot(act_hot, acts[...], 0, 0)
-        yield
+        yield "pre"
         first_norm, first_scale, state = first_norm_step(pre)
-        yield
+        yield "ln1"
         second_norm, second_scale, inner = second_norm_step(state)
-        yield
+        yield "ln2"
         hidden = jnp.maximum(dot(inner, w_one[...], 1, 0), 0.0).astype(BF16)
-        yield
+        yield "hid"
         branch = dot(hidden, w_two[...], 1, 0)
-        yield
+        yield "branch"
         head_norm, head_scale, head = head_norm_step(state, branch)
-        yield
-        logits = dot(moved_ref[span, :], encoder[...], 1, 1)
-        yield
-        (target,) = target_step(logits)
-        yield
+        yield "lnh"
         facts = dot(row_facts, picks[...], 0, 0)
         logits = dot(head, heads[...], 1, 1)
-        yield
-        (grad_logits,) = loss_step(logits, target, facts)
-        yield
+        yield "lg"
+        (grad_logits,) = loss_step(logits, targets[at], facts)
+        yield "lsm"
         grad_head = dot(grad_logits, heads[...], 1, 0)
+        yield "gh"
         head_sums[...] += dot(head, grad_logits, 0, 0)
-        yield
+        yield "hs"
         grad_out, grad_branch, along = head_back_step(grad_head, head_norm, head_scale)
         sums[RUN_GAIN + 16 : RUN_GAIN + 24, :] += add_up(along)
-        yield
+        yield "lbh"
         (grad_zed,) = zed_back_step(dot(grad_branch, w_two[...], 1, 1), hidden)
+        yield "zed"
         sums[RUN_TWO : RUN_TWO + 256, :] += dot(hidden, grad_branch, 0, 0)
-        yield
+        yield "two"
         grad_inner = dot(grad_zed, w_one[...], 1, 1)
+        yield "inn"
         sums[RUN_ONE : RUN_ONE + 256, :] += dot(inner, grad_zed, 0, 0)
-        yield
+        yield "one"
         grad_first, along = block_back_step(grad_inner, second_norm, second_scale, state, grad_out)
         sums[RUN_GAIN + 8 : RUN_GAIN + 16, :] += add_up(along)
-        yield
+        yield "lbb"
         grad_pre, along = first_back_step(grad_first, first_norm, first_scale)
         sums[RUN_GAIN : RUN_GAIN + 8, :] += add_up(along)
-        yield
+        yield "lbf"
         grad_latent[span, :] = dot(grad_pre, w_lat[...], 1, 1)
+        yield "lat"
         sums[RUN_LAT : RUN_LAT + 256, :] += dot(latent, grad_pre, 0, 0)
         sums[RUN_ACT : RUN_ACT + 16, :] += dot(act_hot, grad_pre, 1, 0)
-
-    parts = [one_part(at) for at in range(0, rows, SUB)]
-    turn = 0
-    while any(parts):
-        for at, part in enumerate(parts):
-            if part and turn >= LAG * at and next(part, "end") == "end":
-                parts[at] = None
-        turn += 1
+        yield "lats"
+
+    def one_target(at):
+        logits = dot(moved_ref[at : at + SUB, :], encoder[...], 1, 1)
+        yield "tl"
+        (targets[at],) = target_step(logits)
+        yield "tsm"
+
+    targets = {}
+    parts = [(one_part(at), one_target(at)) for at in range(0, rows, SUB)]
+    for turn in range(len(STAGES) + LAG * (len(parts) - 1)):
+        for at, (part, goal) in enumerate(parts):
+            if 0 <= turn - LAG * at < len(STAGES):
+                for stage in STAGES[turn - LAG * at]:
+                    assert next(goal if stage in ("tl", "tsm") else part) == stage
 
     if not first:
 
@@ -262,10 +287,15 @@
 
     blocks = pl.BlockSpec((ROWS, D), lambda i: (i + at, 0))
     first = before is None
-    in_specs = [pl.BlockSpec(memory_space=pltpu.SMEM), blocks, blocks]
-    in_specs += [pl.BlockSpec((3, 1, ROWS), lambda i: (0, 0, i + at))]
+    if first:
+        moved = pltpu.with_memory_space_constraint(moved, pltpu.VMEM)
+        moved_spec = pl.BlockSpec(memory_space=pltpu.VMEM)
+    else:
+        moved_spec = blocks
+    in_specs = [pl.BlockSpec(memory_space=pltpu.SMEM), blocks, moved_spec]
+    in_specs += [pl.BlockSpec((1, ROWS), lambda i: (0, i + at))] * 3
     in_specs += [whole(w) for w in weights]
-    args = [core, latent, moved, index, *weights]
+    args = [core, latent, moved, *index, *weights]
     scratch = [
         pltpu.VMEM((WIDE, D), BF16),
         pltpu.VMEM((WIDE, D), BF16),
@@ -325,7 +355,7 @@
     swap = [(0, 1), (1, 0)]
     mine = (stay + lax.ppermute(send, "grp", swap).astype(F32)).astype(BF16)
     mine = sum_over_chips(mine)
-    other = lax.ppermute(mine, "grp", swap)
+    other = pltpu.with_memory_space_constraint(lax.ppermute(mine, "grp", swap), pltpu.VMEM)
     sizes = (D, ACTIONS, 1, 1, D, D, 1, CODES, BINS)
     return pl.pallas_call(
         unpack,
@@ -358,8 +388,8 @@
     moved_a = lax.ppermute(future_latent[:ROWS], "grp", swap)
     traj_total = lengths.shape[0] * lax.axis_size("grp") * lax.axis_size("batch")
     steps_idx = jnp.arange(UNROLL, dtype=jnp.int32)
-    mask = (steps_idx[None, :] < lengths[:, None]).astype(jnp.int32).reshape(-1)
-    index = jnp.stack([actions, codes, mask])[:, None, :]
+    mask = (steps_idx[None, :] < lengths[:, None]).astype(jnp.int32).reshape(1, -1)
+    index = (actions[None], codes[None], mask)
     moved_a, index, future_latent = lax.optimization_barrier((moved_a, index, future_latent))
     moved_b = lax.ppermute(future_latent, "grp", swap)
     weights = (

time: 105 us -> 103 us (0.981)
  Pallas kernels: 61.3 us -> 59.8 us
    broadcast_in_dim x1 -> x2, local copies, waits for them, and re-layouts: 0.72 us -> 2.81 us  [body(): index = (actions[None], codes[None], mask)]
    unnamed x6 -> x2, local copies, waits for them, and re-layouts: 1.6 us -> 0.01 us
    another operation x2 -> x0, local copies, waits for them, and re-layouts: 1.59 us -> none  [body(): index = jnp.stack([actions, codes, mask])[:, None, :]]
    pallas_call x2, Pallas kernels: 59 us -> 57.6 us  [run_tower(): pl.pallas_call(functools.partial(tower, scale, first), grid=(steps,), in_...]
  transfers between devices with their start and end apart: 5 -> 5, of which waited for: 3 -> 3; matrix products, arithmetic and copies ran while one was open for 4% -> 5% of each run, Pallas kernels for 10% -> 10%
where the time goes in v3:
time: 103 us; the launch traced here: 102 us
  Pallas kernels  59.8 us (58%)
  blocking collectives  24.3 us (24%)
  waiting for transfers between devices  6.21 us (6%)
  local copies, waits for them, and re-layouts  5.22 us (5%)
  starting transfers between devices  3.79 us (4%)
  other arithmetic  2.28 us (2%)
    pallas_call x2, Pallas kernels, run_tower(): pl.pallas_call(functools.partial(tower, scale, first), grid=(steps,), in_...  57.6 us
    all_to_all x1, blocking collectives, sum_over_chips(): share = swap(mine.reshape(near, -1, D))  14.4 us
    all_to_all x1, blocking collectives, sum_over_chips(): swap(jnp.broadcast_to(share[None], (near, *share.shape))).reshape(rows, D)  9.89 us
    ppermute x1, waiting for transfers between devices, sum_over_chips(): lax.ppermute(share, 'batch', [(i, (i + near) % count) for i in range(coun...  2.92 us
    broadcast_in_dim x2, local copies, waits for them, and re-layouts, body(): index = (actions[None], codes[None], mask)  2.81 us
    ppermute x1, starting transfers between devices, sum_over_chips(): lax.ppermute(share, 'batch', [(i, (i + near) % count) for i in range(coun...  2.66 us
    pallas_call x1, Pallas kernels, finish(): pl.pallas_call(unpack, in_specs=[pl.BlockSpec(memory_space=pltpu.SMEM)] +...  2.22 us
  transfers between devices with their start and end apart: 5, of which 3 were waited for; matrix products, arithmetic and copies ran while one was open for 5% of the time, Pallas kernels for 10%

profile of v3, /device:TPU:0, one launch (start us, length us, event | category | flops | bytes accessed | tf_op | source)
XLA Modules:
  0.0 102.3 jit_solution(10223093281345780442)
XLA Ops:
  0.6 1.1 %slice.3 = bf16[1280,256]{1,0:T(8,128)(2,1)S(1)} slice(bf16[8960,256]{1,0:T(8,128)(2,1)} %param.16), slice={[0:1280], [0:256]} | slice | bytes 1310720 | tf_op jit(solution)/shard_map/slice | solution.py:388
  1.8 0.6 collective-permute-start
  2.3 1.4 %broadcast_in_dim.23.refs_3_ = s32[1,8960]{1,0:T(1,128)} reshape(s32[8960]{0:T(1024)} %param.17) | data formatting | bytes 71680 | tf_op jit(solution)/shard_map/broadcast_in_dim | solution.py:392
  3.7 1.4 %broadcast_in_dim.24.refs_4_ = s32[1,8960]{1,0:T(1,128)} reshape(s32[8960]{0:T(1024)} %param.18) | data formatting | bytes 71680 | tf_op jit(solution)/shard_map/broadcast_in_dim | solution.py:392
  5.2 1.0 fusion
  6.2 1.2 %reshape.62.refs_5_ = s32[1,8960]{1,0:T(1,128)} reshape(s32[1792,5]{1,0:T(8,128)S(1)} %fusion) | data formatting | bytes 71680 | tf_op jit(solution)/shard_map/convert_element_type | solution.py:391
  7.4 0.0 collective-permute-done.refs_2_
  7.4 0.0 collective-permute-start.1
  7.4 9.9 %tower.2 = (f32[8960,256]{1,0:T(8,128)}, f32[256,640]{1,0:T(8,128)}, f32[808,256]{1,0:T(8,128)}) custom-call(s32[1]{0:T(128)} %bitcast.refs_0_.core, bf16[8960,256]{1,0:T(8,128)(2,1)} %refs_1_.3, bf16[1280,256]{1,0:T(8,128)(2,1)S(1)} %collective-permute-done.refs_2_, s32[1,8960]{1,0:T(1,128)} %broadcast_in_dim.23.refs_3_, ...), custom_call_target="tpu_custom_call" | custom-call | flops 3200000000 | bytes 2621440 | tf_op jit(solution)/shard_map/tower/pallas_call | solution.py:315
  17.3 0.0 collective-permute-done.1.refs_2_
  17.3 47.7 %tower.3 = (f32[8960,256]{1,0:T(8,128)}, f32[768,256]{1,0:T(8,128)}, bf16[768,256]{1,0:T(8,128)(2,1)}) custom-call(s32[1]{0:T(128)} %bitcast.refs_0_.core, bf16[8960,256]{1,0:T(8,128)(2,1)} %refs_1_.3, bf16[8960,256]{1,0:T(8,128)(2,1)} %collective-permute-done.1.refs_2_, s32[1,8960]{1,0:T(1,128)} %broadcast_in_dim.23.refs_3_, ...), custom_call_target="tpu_custom_call", output_to_operand_aliasing={{0}: (18, {})} | custom-call | flops 19200000000 | bytes 15728640 | tf_op jit(solution)/shard_map/tower/pallas_call | solution.py:315
  65.0 0.6 collective-permute-start.2
  65.6 1.6 %collective-permute-done.2 = bf16[768,256]{1,0:T(8,128)(2,1)S(1)} collective-permute-done((bf16[768,256]{1,0:T(8,128)(2,1)}, bf16[768,256]{1,0:T(8,128)(2,1)S(1)}, u32[]{:S(2)}, u32[]{:S(2)}) %collective-permute-start.2) | collective-permute-done | bytes 393248 | tf_op jit(solution)/shard_map/ppermute | solution.py:356
  67.2 1.2 %add_convert_fusion = bf16[768,256]{1,0:T(8,128)(2,1)S(1)} fusion(f32[768,256]{1,0:T(8,128)} %get-tuple-element.39, bf16[768,256]{1,0:T(8,128)(2,1)S(1)} %collective-permute-done.2), kind=kLoop, calls=%fused_computation.2 | loop fusion | flops 589824 | bytes 1572864 | tf_op jit(solution)/shard_map/convert_element_type | solution.py:356
  68.4 14.4 %all_to_all.10 = bf16[8,96,256]{2,1,0:T(8,128)(2,1)S(1)} all-to-all(bf16[8,96,256]{2,1,0:T(8,128)(2,1)S(1)} %bitcast.16), channel_id=1, replica_groups={{0,1,2,3,4,5,6,7},{8,9,10,11,12,13,14,15},{16,17,18,19,20,21,22,23},{24..., dimensions={0} | all-to-all | bytes 786432 | tf_op jit(solution)/shard_map/all_to_all | solution.py:346
  82.8 0.1 reduce_sum.12
  82.8 2.7 %collective-permute-start.3 = (bf16[96,256]{1,0:T(8,128)(2,1)S(1)}, bf16[96,256]{1,0:T(8,128)(2,1)S(1)}, u32[]{:S(2)}, u32[]{:S(2)}) collective-permute-start(bf16[96,256]{1,0:T(8,128)(2,1)S(1)} %reduce_sum.12), channel_id=1, source_target_pairs={{0,8},{1,9},{2,10},{3,11},{4,12},{5,13},{6,14},{7,15},{8,0},{9,1},... | collective-permute-start | bytes 147464 | tf_op jit(solution)/shard_map/ppermute | solution.py:349
  85.5 2.9 %collective-permute-done.3 = bf16[96,256]{1,0:T(8,128)(2,1)S(1)} collective-permute-done((bf16[96,256]{1,0:T(8,128)(2,1)S(1)}, bf16[96,256]{1,0:T(8,128)(2,1)S(1)}, u32[]{:S(2)}, u32[]{:S(2)}) %collective-permute-start.3) | collective-permute-done | bytes 49184 | tf_op jit(solution)/shard_map/ppermute | solution.py:349
  88.5 9.9 %all_to_all.11 = bf16[8,96,256]{2,1,0:T(8,128)(2,1)S(1)} all-to-all(bf16[8,96,256]{2,1,0:T(8,128)(2,1)S(1)} %broadcast_in_dim.28), channel_id=1, replica_groups={{0,1,2,3,4,5,6,7},{8,9,10,11,12,13,14,15},{16,17,18,19,20,21,22,23},{24..., dimensions={0} | all-to-all | bytes 786432 | tf_op jit(solution)/shard_map/all_to_all | solution.py:351
  98.3 0.0 copy-start
  98.3 0.0 collective-permute-start.4
  98.3 1.7 %collective-permute-done.4.other = bf16[768,256]{1,0:T(8,128)(2,1)S(1)} collective-permute-done((bf16[768,256]{1,0:T(8,128)(2,1)S(1)}, bf16[768,256]{1,0:T(8,128)(2,1)S(1)}, u32[]{:S(2)}, u32[]{:S(2)}) %collective-permute-start.4) | collective-permute-done | bytes 393248 | tf_op jit(solution)/shard_map/ppermute | solution.py:358
  100.1 0.0 copy-done
  100.1 2.2 %unpack.1 = (f32[256,256]{1,0:T(8,128)}, f32[4,256]{1,0:T(4,128)}, f32[1,256]{1,0:T(1,128)}, f32[1,256]{1,0:T(1,128)}, f32[256,256]{1,0:T(8,128)}, /*index=5*/f3...) custom-call(s32[1]{0:T(128)} %bitcast.refs_0_.core, bf16[768,256]{1,0:T(8,128)(2,1)} %bitcast.15, ...), custom_call_target="tpu_custom_call" | custom-call | tf_op jit(solution)/shard_map/unpack/pallas_call | solution.py:360
  (2 shorter events, 0.0 us)
Async XLA Ops:
  1.8 5.6 %collective-permute-start = (bf16[1280,256]{1,0:T(8,128)(2,1)S(1)}, bf16[1280,256]{1,0:T(8,128)(2,1)S(1)}, u32[]{:S(2)}, u32[]{:S(2)}) collective-permute-start(bf16[1280,256]{1,0:T(8,128)(2,1)S(1)} %slice.3), channel_id=1, source_target_pairs={{0,16},{16,0},{1,17},{17,1},{2,18},{18,2},{3,19},{19,3},{4,20},{20... | collective-permute-start | bytes 1966088 | tf_op jit(solution)/shard_map/ppermute | solution.py:388
  7.4 9.9 %collective-permute-start.1 = (bf16[8960,256]{1,0:T(8,128)(2,1)}, bf16[8960,256]{1,0:T(8,128)(2,1)}, u32[]{:S(2)}, u32[]{:S(2)}) collective-permute-start(bf16[8960,256]{1,0:T(8,128)(2,1)} %param.16), channel_id=1, source_target_pairs={{0,16},{16,0},{1,17},{17,1},{2,18},{18,2},{3,19},{19,3},{4,20},{20... | collective-permute-start | bytes 13762568 | tf_op jit(solution)/shard_map/ppermute | solution.py:394
  65.0 2.1 %collective-permute-start.2 = (bf16[768,256]{1,0:T(8,128)(2,1)}, bf16[768,256]{1,0:T(8,128)(2,1)S(1)}, u32[]{:S(2)}, u32[]{:S(2)}) collective-permute-start(bf16[768,256]{1,0:T(8,128)(2,1)} %get-tuple-element.40), channel_id=1, source_target_pairs={{0,16},{16,0},{1,17},{17,1},{2,18},{18,2},{3,19},{19,3},{4,20},{20... | collective-permute-start | bytes 1179656 | tf_op jit(solution)/shard_map/ppermute | solution.py:356
  82.8 5.6 %collective-permute-start.3 = (bf16[96,256]{1,0:T(8,128)(2,1)S(1)}, bf16[96,256]{1,0:T(8,128)(2,1)S(1)}, u32[]{:S(2)}, u32[]{:S(2)}) collective-permute-start(bf16[96,256]{1,0:T(8,128)(2,1)S(1)} %reduce_sum.12), channel_id=1, source_target_pairs={{0,8},{1,9},{2,10},{3,11},{4,12},{5,13},{6,14},{7,15},{8,0},{9,1},... | collective-permute-start | bytes 147464 | tf_op jit(solution)/shard_map/ppermute | solution.py:349
  98.3 1.7 %copy-start = (bf16[8,96,256]{2,1,0:T(8,128)(2,1)}, bf16[8,96,256]{2,1,0:T(8,128)(2,1)S(1)}, u32[]{:S(2)}) copy-start(bf16[8,96,256]{2,1,0:T(8,128)(2,1)S(1)} %all_to_all.11) | copy-start | bytes 1179652
  98.3 1.7 %collective-permute-start.4 = (bf16[768,256]{1,0:T(8,128)(2,1)S(1)}, bf16[768,256]{1,0:T(8,128)(2,1)S(1)}, u32[]{:S(2)}, u32[]{:S(2)}) collective-permute-start(bf16[768,256]{1,0:T(8,128)(2,1)S(1)} %bitcast.14), channel_id=1, source_target_pairs={{0,16},{16,0},{1,17},{17,1},{2,18},{18,2},{3,19},{19,3},{4,20},{20... | collective-permute-start | bytes 1179656 | tf_op jit(solution)/shard_map/ppermute | solution.py:358

commit v4 on v3

--- a/solution.py
+++ b/solution.py
@@ -18,25 +18,11 @@
 CODE_AT = WIDE - CODES
 ROWS = 1280
 SUB = 640
-LAG = 6
-STAGES = (
-    ("tl",),
-    ("pre",),
-    ("ln1",),
-    ("ln2",),
-    ("hid",),
-    ("branch",),
-    ("lnh",),
-    ("tsm",),
-    ("lg",),
-    ("lsm",),
-    ("gh", "hs"),
-    ("lbh",),
-    ("zed", "two"),
-    ("inn", "one"),
-    ("lbb",),
-    ("lbf",),
-    ("lat", "lats"),
+ORDER = (
+    "Atl", "Apre", "Aln1", "Aln2", "Ahid", "Atsm", "Abranch", "Alnh", "Bpre", "Bln1", "Alg",
+    "Btl", "Alsm", "Bln2", "Agh", "Ahs", "Bhid", "Albh", "Btsm", "Bbranch", "Azed", "Atwo",
+    "Blnh", "Ainn", "Aone", "Albb", "Blg", "Albf", "Alat", "Alats", "Blsm", "Bgh", "Bhs",
+    "Blbh", "Bzed", "Btwo", "Binn", "Bone", "Blbb", "Blbf", "Blat", "Blats",
 )
 F32 = jnp.float32
 BF16 = jnp.bfloat16
@@ -96,14 +82,14 @@
     return exps, jnp.sum(functools.reduce(jnp.add, exps), axis=1, keepdims=True)
 
 
-def tower(scale, first, *refs):
-    (core, latent_ref, moved_ref, action_ref, code_ref, mask_ref) = refs[:6]
+def tower(scale, first, first_block, *refs):
+    (core, latent_ref, moved_ref, action_ref, code_ref, length_ref) = refs[:6]
     (w_lat, w_act, gain_in, gain_bl, gain_he, w_one, w_two, w_chance, w_value, w_target) = refs[6:16]
     if first:
-        grad_latent, head_sums, sums, heads, encoder, acts, picks = refs[16:]
+        grad_latent, head_sums, sums, heads, encoder, acts, picks, spread = refs[16:]
     else:
         head_before, before, _, grad_latent, stay, send = refs[16:22]
-        heads, encoder, acts, picks, head_sums, sums, packed = refs[22:]
+        heads, encoder, acts, picks, spread, head_sums, sums, packed = refs[22:]
     rows = latent_ref.shape[0]
 
     @pl.when(pl.program_id(0) == 0)
@@ -122,6 +108,9 @@
         col = lax.broadcasted_iota(jnp.int32, (48, D), 1)
         coded = (row < CODES) & (col == row + 128 - CODES)
         picks[...] = jnp.where(coded | ((row == CODES) & (col >= 128)), 1.0, 0.0).astype(BF16)
+        row = UNROLL * lax.broadcasted_iota(jnp.int32, (128, SUB), 0)
+        col = lax.broadcasted_iota(jnp.int32, (128, SUB), 1)
+        spread[...] = jnp.where((col >= row) & (col < row + UNROLL), 1.0, 0.0).astype(BF16)
         head_sums[...] = jnp.zeros_like(head_sums) if first else head_before[...]
         sums[...] = jnp.zeros_like(sums) if first else before[...]
 
@@ -137,12 +126,22 @@
 
     def one_part(at):
         span = slice(at, at + SUB)
-        act_hot = lax.broadcasted_iota(jnp.int32, (16, SUB), 0) == action_ref[:, span]
+        block = pl.program_id(0) + first_block
+        lines = block * (rows // 128) + at // 128
+        actions = jnp.concatenate(
+            [action_ref[pl.ds(lines + i, 1), :] for i in range(SUB // 128)], axis=1
+        )
+        codes = jnp.concatenate(
+            [code_ref[pl.ds(lines + i, 1), :] for i in range(SUB // 128)], axis=1
+        )
+        lengths = length_ref[pl.ds(block * (rows // SUB) + at // SUB, 1), :].astype(F32)
+        lengths = dot(jnp.broadcast_to(lengths, (16, 128)).astype(BF16), spread[...], 1, 0)[0:1]
+        unrolled = lax.rem(lax.broadcasted_iota(jnp.int32, (1, SUB), 1), UNROLL).astype(F32)
+        mask = (unrolled < lengths).astype(F32)
+        act_hot = lax.broadcasted_iota(jnp.int32, (16, SUB), 0) == actions
         act_hot = act_hot.astype(F32).astype(BF16)
         kind = lax.broadcasted_iota(jnp.int32, (48, SUB), 0)
-        row_facts = jnp.where(
-            kind == CODES, mask_ref[:, span].astype(F32), (kind == code_ref[:, span]).astype(F32)
-        ).astype(BF16)
+        row_facts = jnp.where(kind == CODES, mask, (kind == codes).astype(F32)).astype(BF16)
 
         latent = latent_ref[span, :]
         def first_norm_step(pre):
@@ -236,12 +235,11 @@
         yield "tsm"
 
     targets = {}
-    parts = [(one_part(at), one_target(at)) for at in range(0, rows, SUB)]
-    for turn in range(len(STAGES) + LAG * (len(parts) - 1)):
-        for at, (part, goal) in enumerate(parts):
-            if 0 <= turn - LAG * at < len(STAGES):
-                for stage in STAGES[turn - LAG * at]:
-                    assert next(goal if stage in ("tl", "tsm") else part) == stage
+    parts = {name: one_part(at) for name, at in zip("AB", range(0, rows, SUB))}
+    goals = {name: one_target(at) for name, at in zip("AB", range(0, rows, SUB))}
+    for word in ORDER:
+        stages = goals if word[1:] in ("tl", "tsm") else parts
+        assert next(stages[word[0]]) == word[1:]
 
     if not first:
 
@@ -293,7 +291,7 @@
     else:
         moved_spec = blocks
     in_specs = [pl.BlockSpec(memory_space=pltpu.SMEM), blocks, moved_spec]
-    in_specs += [pl.BlockSpec((1, ROWS), lambda i: (0, i + at))] * 3
+    in_specs += [whole(part) for part in index]
     in_specs += [whole(w) for w in weights]
     args = [core, latent, moved, *index, *weights]
     scratch = [
@@ -301,22 +299,24 @@
         pltpu.VMEM((WIDE, D), BF16),
         pltpu.VMEM((16, D), BF16),
         pltpu.VMEM((48, D), BF16),
+        pltpu.VMEM((128, SUB), BF16),
     ]
     aliases = {}
     if first:
-        results = [shape(D, WIDE), shape(RUNNING, D)]
+        results = [pltpu.VMEM((D, WIDE), F32), pltpu.VMEM((RUNNING, D), F32)]
     else:
-        results = [shape(HALF, D), shape(HALF, D, BF16)]
+        results = [pltpu.VMEM((HALF, D), F32), pltpu.VMEM((HALF, D), BF16)]
         scratch += [pltpu.VMEM((D, WIDE), F32), pltpu.VMEM((RUNNING, D), F32)]
         scratch += [pltpu.VMEM((PACKED, D), F32)]
-        in_specs += [whole(before[1]), whole(before[2]), pl.BlockSpec(memory_space=pl.ANY)]
-        args += [before[1], before[2], before[0]]
+        in_specs += [pl.BlockSpec(memory_space=pltpu.VMEM)] * 2 + [pl.BlockSpec(memory_space=pl.ANY)]
+        args += [pltpu.with_memory_space_constraint(b, pltpu.VMEM) for b in before[1:]]
+        args += [before[0]]
         aliases = {len(args) - 1: 0}
     return pl.pallas_call(
-        functools.partial(tower, scale, first),
+        functools.partial(tower, scale, first, at),
         grid=(steps,),
         in_specs=in_specs,
-        out_specs=[blocks] + [whole(r) for r in results],
+        out_specs=[blocks] + [pl.BlockSpec(memory_space=pltpu.VMEM)] * 2,
         out_shape=[shape(rows, D)] + results,
         scratch_shapes=scratch,
         input_output_aliases=aliases,
@@ -387,10 +387,8 @@
     swap = [(0, 1), (1, 0)]
     moved_a = lax.ppermute(future_latent[:ROWS], "grp", swap)
     traj_total = lengths.shape[0] * lax.axis_size("grp") * lax.axis_size("batch")
-    steps_idx = jnp.arange(UNROLL, dtype=jnp.int32)
-    mask = (steps_idx[None, :] < lengths[:, None]).astype(jnp.int32).reshape(1, -1)
-    index = (actions[None], codes[None], mask)
-    moved_a, index, future_latent = lax.optimization_barrier((moved_a, index, future_latent))
+    index = (actions.reshape(-1, 128), codes.reshape(-1, 128), lengths.reshape(-1, SUB // UNROLL))
+    moved_a, future_latent = lax.optimization_barrier((moved_a, future_latent))
     moved_b = lax.ppermute(future_latent, "grp", swap)
     weights = (
         w_lat,

time: 103 us -> 98.7 us (0.958)
  local copies, waits for them, and re-layouts: 5.22 us -> 1.16 us
  other arithmetic: 2.28 us -> 0.19 us
  waiting for transfers between devices: 6.21 us -> 7.96 us
    broadcast_in_dim x2 -> x0, local copies, waits for them, and re-layouts: 2.81 us -> none  [body(): index = (actions[None], codes[None], mask)]
    ppermute x1, waiting for transfers between devices: 0.01 us -> 1.72 us  [body(): moved_a = lax.ppermute(future_latent[:ROWS], 'grp', swap)]
    convert_element_type x1 -> x0, local copies, waits for them, and re-layouts: 1.24 us -> none  [body(): (steps_idx[None, :] < lengths[:, None]).astype(jnp.int32).reshape(1, -1)]
    convert_element_type x1, other arithmetic: 1.22 us -> 0.12 us  [finish(): mine = (stay + lax.ppermute(send, 'grp', swap).astype(F32)).astype(BF16)]
  transfers between devices with their start and end apart: 5 -> 5, of which waited for: 3 -> 4; matrix products, arithmetic and copies ran while one was open for 5% -> 0% of each run, Pallas kernels for 10% -> 10%
where the time goes in v4:
time: 98.7 us; the launch traced here: 98.4 us
  Pallas kernels  60.4 us (61%)
  blocking collectives  24.3 us (25%)
  waiting for transfers between devices  7.96 us (8%)
  starting transfers between devices  3.72 us (4%)
  local copies, waits for them, and re-layouts  1.16 us (1%)
    pallas_call x2, Pallas kernels, run_tower(): pl.pallas_call(functools.partial(tower, scale, first, at), grid=(steps,),...  58.2 us
    all_to_all x1, blocking collectives, sum_over_chips(): share = swap(mine.reshape(near, -1, D))  14.4 us
    all_to_all x1, blocking collectives, sum_over_chips(): swap(jnp.broadcast_to(share[None], (near, *share.shape))).reshape(rows, D)  9.89 us
    ppermute x1, waiting for transfers between devices, sum_over_chips(): lax.ppermute(share, 'batch', [(i, (i + near) % count) for i in range(coun...  2.92 us
    ppermute x1, starting transfers between devices, sum_over_chips(): lax.ppermute(share, 'batch', [(i, (i + near) % count) for i in range(coun...  2.66 us
    pallas_call x1, Pallas kernels, finish(): pl.pallas_call(unpack, in_specs=[pl.BlockSpec(memory_space=pltpu.SMEM)] +...  2.22 us
  transfers between devices with their start and end apart: 5, of which 4 were waited for; matrix products, arithmetic and copies ran while one was open for 0% of the time, Pallas kernels for 10%

profile of v4, /device:TPU:0, one launch (start us, length us, event | category | flops | bytes accessed | tf_op | source)
XLA Modules:
  0.0 98.4 jit_solution(16852072811048673990)
XLA Ops:
  0.6 1.1 %slice.3 = bf16[1280,256]{1,0:T(8,128)(2,1)S(1)} slice(bf16[8960,256]{1,0:T(8,128)(2,1)} %param.16), slice={[0:1280], [0:256]} | slice | bytes 1310720 | tf_op jit(solution)/shard_map/slice | solution.py:388
  1.8 0.6 collective-permute-start
  2.3 1.7 %collective-permute-done.refs_2_ = bf16[1280,256]{1,0:T(8,128)(2,1)S(1)} collective-permute-done((bf16[1280,256]{1,0:T(8,128)(2,1)S(1)}, bf16[1280,256]{1,0:T(8,128)(2,1)S(1)}, u32[]{:S(2)}, u32[]{:S(2)}) %collective-permute-start) | collective-permute-done | bytes 655392 | tf_op jit(solution)/shard_map/ppermute | solution.py:388
  4.1 0.4 collective-permute-start.1
  4.4 10.0 %tower.2 = (f32[8960,256]{1,0:T(8,128)}, f32[256,640]{1,0:T(8,128)S(1)}, f32[808,256]{1,0:T(8,128)S(1)}) custom-call(s32[1]{0:T(128)} %bitcast.refs_0_.core, bf16[8960,256]{1,0:T(8,128)(2,1)} %refs_1_.3, bf16[1280,256]{1,0:T(8,128)(2,1)S(1)} %collective-permute-done.refs_2_, s32[70,128]{1,0:T(8,128)} %bitcast.25, s32[70,128]{1,0:T(8,128)} %bitcast.27, ...), custom_call_target="tpu_custom_call" | custom-call | flops 3200000000 | bytes 2621440 | tf_op jit(solution)/shard_map/tower/pallas_call | solution.py:315
  14.4 0.0 collective-permute-done.1.refs_2_
  14.4 48.2 %tower.3 = (f32[8960,256]{1,0:T(8,128)}, f32[768,256]{1,0:T(8,128)S(1)}, bf16[768,256]{1,0:T(8,128)(2,1)S(1)}) custom-call(s32[1]{0:T(128)} %bitcast.refs_0_.core, bf16[8960,256]{1,0:T(8,128)(2,1)} %refs_1_.3, bf16[8960,256]{1,0:T(8,128)(2,1)} %collective-permute-done.1.refs_2_, s32[70,128]{1,0:T(8,128)} %bitcast.26, ...), custom_call_target="tpu_custom_call", output_to_operand_aliasing={{0}: (18, {})} | custom-call | flops 19200000000 | bytes 15728640 | tf_op jit(solution)/shard_map/tower/pallas_call | solution.py:315
  62.6 0.1 collective-permute-start.2
  62.8 1.6 %collective-permute-done.2 = bf16[768,256]{1,0:T(8,128)(2,1)S(1)} collective-permute-done((bf16[768,256]{1,0:T(8,128)(2,1)S(1)}, bf16[768,256]{1,0:T(8,128)(2,1)S(1)}, u32[]{:S(2)}, u32[]{:S(2)}) %collective-permute-start.2) | collective-permute-done | bytes 393248 | tf_op jit(solution)/shard_map/ppermute | solution.py:356
  64.4 0.1 add_convert_fusion
  64.5 14.4 %all_to_all.10 = bf16[8,96,256]{2,1,0:T(8,128)(2,1)S(1)} all-to-all(bf16[8,96,256]{2,1,0:T(8,128)(2,1)S(1)} %bitcast.19), channel_id=1, replica_groups={{0,1,2,3,4,5,6,7},{8,9,10,11,12,13,14,15},{16,17,18,19,20,21,22,23},{24..., dimensions={0} | all-to-all | bytes 786432 | tf_op jit(solution)/shard_map/all_to_all | solution.py:346
  78.9 0.1 reduce_sum.12
  78.9 2.7 %collective-permute-start.3 = (bf16[96,256]{1,0:T(8,128)(2,1)S(1)}, bf16[96,256]{1,0:T(8,128)(2,1)S(1)}, u32[]{:S(2)}, u32[]{:S(2)}) collective-permute-start(bf16[96,256]{1,0:T(8,128)(2,1)S(1)} %reduce_sum.12), channel_id=1, source_target_pairs={{0,8},{1,9},{2,10},{3,11},{4,12},{5,13},{6,14},{7,15},{8,0},{9,1},... | collective-permute-start | bytes 147464 | tf_op jit(solution)/shard_map/ppermute | solution.py:349
  81.6 2.9 %collective-permute-done.3 = bf16[96,256]{1,0:T(8,128)(2,1)S(1)} collective-permute-done((bf16[96,256]{1,0:T(8,128)(2,1)S(1)}, bf16[96,256]{1,0:T(8,128)(2,1)S(1)}, u32[]{:S(2)}, u32[]{:S(2)}) %collective-permute-start.3) | collective-permute-done | bytes 49184 | tf_op jit(solution)/shard_map/ppermute | solution.py:349
  84.6 9.9 %all_to_all.11 = bf16[8,96,256]{2,1,0:T(8,128)(2,1)S(1)} all-to-all(bf16[8,96,256]{2,1,0:T(8,128)(2,1)S(1)} %broadcast_in_dim.18), channel_id=1, replica_groups={{0,1,2,3,4,5,6,7},{8,9,10,11,12,13,14,15},{16,17,18,19,20,21,22,23},{24..., dimensions={0} | all-to-all | bytes 786432 | tf_op jit(solution)/shard_map/all_to_all | solution.py:351
  94.5 0.0 copy-start
  94.5 0.0 collective-permute-start.4
  94.5 1.7 %collective-permute-done.4.other = bf16[768,256]{1,0:T(8,128)(2,1)S(1)} collective-permute-done((bf16[768,256]{1,0:T(8,128)(2,1)S(1)}, bf16[768,256]{1,0:T(8,128)(2,1)S(1)}, u32[]{:S(2)}, u32[]{:S(2)}) %collective-permute-start.4) | collective-permute-done | bytes 393248 | tf_op jit(solution)/shard_map/ppermute | solution.py:358
  96.2 0.0 copy-done
  96.2 2.2 %unpack.1 = (f32[256,256]{1,0:T(8,128)}, f32[4,256]{1,0:T(4,128)}, f32[1,256]{1,0:T(1,128)}, f32[1,256]{1,0:T(1,128)}, f32[256,256]{1,0:T(8,128)}, /*index=5*/f3...) custom-call(s32[1]{0:T(128)} %bitcast.refs_0_.core, bf16[768,256]{1,0:T(8,128)(2,1)} %bitcast.18, ...), custom_call_target="tpu_custom_call" | custom-call | tf_op jit(solution)/shard_map/unpack/pallas_call | solution.py:360
  (2 shorter events, 0.0 us)
Async XLA Ops:
  1.8 2.3 %collective-permute-start = (bf16[1280,256]{1,0:T(8,128)(2,1)S(1)}, bf16[1280,256]{1,0:T(8,128)(2,1)S(1)}, u32[]{:S(2)}, u32[]{:S(2)}) collective-permute-start(bf16[1280,256]{1,0:T(8,128)(2,1)S(1)} %slice.3), channel_id=1, source_target_pairs={{0,16},{16,0},{1,17},{17,1},{2,18},{18,2},{3,19},{19,3},{4,20},{20... | collective-permute-start | bytes 1966088 | tf_op jit(solution)/shard_map/ppermute | solution.py:388
  4.1 10.4 %collective-permute-start.1 = (bf16[8960,256]{1,0:T(8,128)(2,1)}, bf16[8960,256]{1,0:T(8,128)(2,1)}, u32[]{:S(2)}, u32[]{:S(2)}) collective-permute-start(bf16[8960,256]{1,0:T(8,128)(2,1)} %param.16), channel_id=1, source_target_pairs={{0,16},{16,0},{1,17},{17,1},{2,18},{18,2},{3,19},{19,3},{4,20},{20... | collective-permute-start | bytes 13762568 | tf_op jit(solution)/shard_map/ppermute | solution.py:392
  62.6 1.7 %collective-permute-start.2 = (bf16[768,256]{1,0:T(8,128)(2,1)S(1)}, bf16[768,256]{1,0:T(8,128)(2,1)S(1)}, u32[]{:S(2)}, u32[]{:S(2)}) collective-permute-start(bf16[768,256]{1,0:T(8,128)(2,1)S(1)} %get-tuple-element.34), channel_id=1, source_target_pairs={{0,16},{16,0},{1,17},{17,1},{2,18},{18,2},{3,19},{19,3},{4,20},{20... | collective-permute-start | bytes 1179656 | tf_op jit(solution)/shard_map/ppermute | solution.py:356
  78.9 5.6 %collective-permute-start.3 = (bf16[96,256]{1,0:T(8,128)(2,1)S(1)}, bf16[96,256]{1,0:T(8,128)(2,1)S(1)}, u32[]{:S(2)}, u32[]{:S(2)}) collective-permute-start(bf16[96,256]{1,0:T(8,128)(2,1)S(1)} %reduce_sum.12), channel_id=1, source_target_pairs={{0,8},{1,9},{2,10},{3,11},{4,12},{5,13},{6,14},{7,15},{8,0},{9,1},... | collective-permute-start | bytes 147464 | tf_op jit(solution)/shard_map/ppermute | solution.py:349
  94.5 1.7 %copy-start = (bf16[8,96,256]{2,1,0:T(8,128)(2,1)}, bf16[8,96,256]{2,1,0:T(8,128)(2,1)S(1)}, u32[]{:S(2)}) copy-start(bf16[8,96,256]{2,1,0:T(8,128)(2,1)S(1)} %all_to_all.11) | copy-start | bytes 1179652
  94.5 1.7 %collective-permute-start.4 = (bf16[768,256]{1,0:T(8,128)(2,1)S(1)}, bf16[768,256]{1,0:T(8,128)(2,1)S(1)}, u32[]{:S(2)}, u32[]{:S(2)}) collective-permute-start(bf16[768,256]{1,0:T(8,128)(2,1)S(1)} %bitcast.17), channel_id=1, source_target_pairs={{0,16},{16,0},{1,17},{17,1},{2,18},{18,2},{3,19},{19,3},{4,20},{20... | collective-permute-start | bytes 1179656 | tf_op jit(solution)/shard_map/ppermute | solution.py:358

commit v5 on v4

--- a/solution.py
+++ b/solution.py
@@ -20,9 +20,9 @@
 SUB = 640
 ORDER = (
     "Atl", "Apre", "Aln1", "Aln2", "Ahid", "Atsm", "Abranch", "Alnh", "Bpre", "Bln1", "Alg",
-    "Btl", "Alsm", "Bln2", "Agh", "Ahs", "Bhid", "Albh", "Btsm", "Bbranch", "Azed", "Atwo",
-    "Blnh", "Ainn", "Aone", "Albb", "Blg", "Albf", "Alat", "Alats", "Blsm", "Bgh", "Bhs",
-    "Blbh", "Bzed", "Btwo", "Binn", "Bone", "Blbb", "Blbf", "Blat", "Blats",
+    "Btl", "Alsm", "facts", "Bln2", "Agh", "Ahs", "Bhid", "Albh", "Btsm", "Bbranch", "Azed",
+    "Atwo", "Blnh", "Ainn", "Aone", "Albb", "Blg", "Albf", "Alat", "Alats", "Blsm", "Bgh",
+    "Bhs", "Blbh", "Bzed", "Btwo", "Binn", "Bone", "Blbb", "Blbf", "Blat", "Blats",
 )
 F32 = jnp.float32
 BF16 = jnp.bfloat16
@@ -82,14 +82,15 @@
     return exps, jnp.sum(functools.reduce(jnp.add, exps), axis=1, keepdims=True)
 
 
-def tower(scale, first, first_block, *refs):
+def tower(scale, first, first_block, last_block, *refs):
     (core, latent_ref, moved_ref, action_ref, code_ref, length_ref) = refs[:6]
     (w_lat, w_act, gain_in, gain_bl, gain_he, w_one, w_two, w_chance, w_value, w_target) = refs[6:16]
     if first:
-        grad_latent, head_sums, sums, heads, encoder, acts, picks, spread = refs[16:]
+        grad_latent, head_sums, sums, heads, encoder, acts, picks, spread = refs[16:24]
+        act_hots, facts_kept = refs[24:]
     else:
         head_before, before, _, grad_latent, stay, send = refs[16:22]
-        heads, encoder, acts, picks, spread, head_sums, sums, packed = refs[22:]
+        heads, encoder, acts, picks, spread, act_hots, facts_kept, head_sums, sums, packed = refs[22:]
     rows = latent_ref.shape[0]
 
     @pl.when(pl.program_id(0) == 0)
@@ -124,25 +125,40 @@
         share = 1.0 / total
         return (jnp.concatenate([(e * share).astype(BF16) for e in exps], axis=1),)
 
+    now = lax.rem(pl.program_id(0), 2)
+
+    def keep_facts(block, slot):
+        for at in range(0, rows, SUB):
+            span = slice(at, at + SUB)
+            lines = block * (rows // 128) + at // 128
+            actions = jnp.concatenate(
+                [action_ref[pl.ds(lines + i, 1), :] for i in range(SUB // 128)], axis=1
+            )
+            codes = jnp.concatenate(
+                [code_ref[pl.ds(lines + i, 1), :] for i in range(SUB // 128)], axis=1
+            )
+            lengths = length_ref[pl.ds(block * (rows // SUB) + at // SUB, 1), :].astype(F32)
+            lengths = jnp.broadcast_to(lengths, (16, 128)).astype(BF16)
+            lengths = dot(lengths, spread[...], 1, 0)[0:1]
+            unrolled = lax.rem(lax.broadcasted_iota(jnp.int32, (1, SUB), 1), UNROLL).astype(F32)
+            mask = (unrolled < lengths).astype(F32)
+            hot = lax.broadcasted_iota(jnp.int32, (16, SUB), 0) == actions
+            act_hots[slot, :, span] = hot.astype(F32).astype(BF16)
+            kind = lax.broadcasted_iota(jnp.int32, (48, SUB), 0)
+            facts_kept[slot, :, span] = jnp.where(
+                kind == CODES, mask, (kind == codes).astype(F32)
+            ).astype(BF16)
+
+    this_block = pl.program_id(0) + first_block
+
+    @pl.when(pl.program_id(0) == 0)
+    def _():
+        keep_facts(this_block, now)
+
     def one_part(at):
         span = slice(at, at + SUB)
-        block = pl.program_id(0) + first_block
-        lines = block * (rows // 128) + at // 128
-        actions = jnp.concatenate(
-            [action_ref[pl.ds(lines + i, 1), :] for i in range(SUB // 128)], axis=1
-        )
-        codes = jnp.concatenate(
-            [code_ref[pl.ds(lines + i, 1), :] for i in range(SUB // 128)], axis=1
-        )
-        lengths = length_ref[pl.ds(block * (rows // SUB) + at // SUB, 1), :].astype(F32)
-        lengths = dot(jnp.broadcast_to(lengths, (16, 128)).astype(BF16), spread[...], 1, 0)[0:1]
-        unrolled = lax.rem(lax.broadcasted_iota(jnp.int32, (1, SUB), 1), UNROLL).astype(F32)
-        mask = (unrolled < lengths).astype(F32)
-        act_hot = lax.broadcasted_iota(jnp.int32, (16, SUB), 0) == actions
-        act_hot = act_hot.astype(F32).astype(BF16)
-        kind = lax.broadcasted_iota(jnp.int32, (48, SUB), 0)
-        row_facts = jnp.where(kind == CODES, mask, (kind == codes).astype(F32)).astype(BF16)
-
+        act_hot = act_hots[now, :, span]
+        row_facts = facts_kept[now, :, span]
         latent = latent_ref[span, :]
         def first_norm_step(pre):
             normed, scaled = normalize(pre)
@@ -238,6 +254,10 @@
     parts = {name: one_part(at) for name, at in zip("AB", range(0, rows, SUB))}
     goals = {name: one_target(at) for name, at in zip("AB", range(0, rows, SUB))}
     for word in ORDER:
+        if word == "facts":
+            if not first:
+                keep_facts(jnp.minimum(this_block + 1, last_block), 1 - now)
+            continue
         stages = goals if word[1:] in ("tl", "tsm") else parts
         assert next(stages[word[0]]) == word[1:]
 
@@ -300,6 +320,8 @@
         pltpu.VMEM((16, D), BF16),
         pltpu.VMEM((48, D), BF16),
         pltpu.VMEM((128, SUB), BF16),
+        pltpu.VMEM((2, 16, ROWS), BF16),
+        pltpu.VMEM((2, 48, ROWS), BF16),
     ]
     aliases = {}
     if first:
@@ -313,7 +335,7 @@
         args += [before[0]]
         aliases = {len(args) - 1: 0}
     return pl.pallas_call(
-        functools.partial(tower, scale, first, at),
+        functools.partial(tower, scale, first, at, at + steps - 1),
         grid=(steps,),
         in_specs=in_specs,
         out_specs=[blocks] + [pl.BlockSpec(memory_space=pltpu.VMEM)] * 2,

time: 98.7 us -> 96.4 us (0.977)
  Pallas kernels: 60.4 us -> 58.1 us
    pallas_call x2, Pallas kernels: 58.2 us -> 55.9 us  [run_tower(): pl.pallas_call(functools.partial(tower, scale, first, at, at + steps - 1)...]
where the time goes in v5:
time: 96.4 us; the launch traced here: 96.1 us
  Pallas kernels  58.1 us (60%)
  blocking collectives  24.3 us (25%)
  waiting for transfers between devices  7.95 us (8%)
  starting transfers between devices  3.74 us (4%)
  local copies, waits for them, and re-layouts  1.16 us (1%)
    pallas_call x2, Pallas kernels, run_tower(): pl.pallas_call(functools.partial(tower, scale, first, at, at + steps - 1)...  55.9 us
    all_to_all x1, blocking collectives, sum_over_chips(): share = swap(mine.reshape(near, -1, D))  14.4 us
    all_to_all x1, blocking collectives, sum_over_chips(): swap(jnp.broadcast_to(share[None], (near, *share.shape))).reshape(rows, D)  9.89 us
    ppermute x1, waiting for transfers between devices, sum_over_chips(): lax.ppermute(share, 'batch', [(i, (i + near) % count) for i in range(coun...  2.92 us
    ppermute x1, starting transfers between devices, sum_over_chips(): lax.ppermute(share, 'batch', [(i, (i + near) % count) for i in range(coun...  2.66 us
    pallas_call x1, Pallas kernels, finish(): pl.pallas_call(unpack, in_specs=[pl.BlockSpec(memory_space=pltpu.SMEM)] +...  2.22 us
  transfers between devices with their start and end apart: 5, of which 4 were waited for; matrix products, arithmetic and copies ran while one was open for 0% of the time, Pallas kernels for 10%

profile of v5, /device:TPU:0, one launch (start us, length us, event | category | flops | bytes accessed | tf_op | source)
XLA Modules:
  0.0 96.1 jit_solution(18161875948364470923)
XLA Ops:
  0.6 1.1 %slice.3 = bf16[1280,256]{1,0:T(8,128)(2,1)S(1)} slice(bf16[8960,256]{1,0:T(8,128)(2,1)} %param.16), slice={[0:1280], [0:256]} | slice | bytes 1310720 | tf_op jit(solution)/shard_map/slice | solution.py:410
  1.8 0.6 collective-permute-start
  2.3 1.7 %collective-permute-done.refs_2_ = bf16[1280,256]{1,0:T(8,128)(2,1)S(1)} collective-permute-done((bf16[1280,256]{1,0:T(8,128)(2,1)S(1)}, bf16[1280,256]{1,0:T(8,128)(2,1)S(1)}, u32[]{:S(2)}, u32[]{:S(2)}) %collective-permute-start) | collective-permute-done | bytes 655392 | tf_op jit(solution)/shard_map/ppermute | solution.py:410
  4.1 0.4 collective-permute-start.1
  4.4 9.7 %tower.2 = (f32[8960,256]{1,0:T(8,128)}, f32[256,640]{1,0:T(8,128)S(1)}, f32[808,256]{1,0:T(8,128)S(1)}) custom-call(s32[1]{0:T(128)} %bitcast.refs_0_.core, bf16[8960,256]{1,0:T(8,128)(2,1)} %refs_1_.3, bf16[1280,256]{1,0:T(8,128)(2,1)S(1)} %collective-permute-done.refs_2_, s32[70,128]{1,0:T(8,128)} %bitcast.25, s32[70,128]{1,0:T(8,128)} %bitcast.27, ...), custom_call_target="tpu_custom_call" | custom-call | flops 3200000000 | bytes 2621440 | tf_op jit(solution)/shard_map/tower/pallas_call | solution.py:337
  14.2 0.0 collective-permute-done.1.refs_2_
  14.2 46.1 %tower.3 = (f32[8960,256]{1,0:T(8,128)}, f32[768,256]{1,0:T(8,128)S(1)}, bf16[768,256]{1,0:T(8,128)(2,1)S(1)}) custom-call(s32[1]{0:T(128)} %bitcast.refs_0_.core, bf16[8960,256]{1,0:T(8,128)(2,1)} %refs_1_.3, bf16[8960,256]{1,0:T(8,128)(2,1)} %collective-permute-done.1.refs_2_, s32[70,128]{1,0:T(8,128)} %bitcast.26, ...), custom_call_target="tpu_custom_call", output_to_operand_aliasing={{0}: (18, {})} | custom-call | flops 19200000000 | bytes 15728640 | tf_op jit(solution)/shard_map/tower/pallas_call | solution.py:337
  60.3 0.1 collective-permute-start.2
  60.4 1.6 %collective-permute-done.2 = bf16[768,256]{1,0:T(8,128)(2,1)S(1)} collective-permute-done((bf16[768,256]{1,0:T(8,128)(2,1)S(1)}, bf16[768,256]{1,0:T(8,128)(2,1)S(1)}, u32[]{:S(2)}, u32[]{:S(2)}) %collective-permute-start.2) | collective-permute-done | bytes 393248 | tf_op jit(solution)/shard_map/ppermute | solution.py:378
  62.0 0.1 add_convert_fusion
  62.1 14.4 %all_to_all.10 = bf16[8,96,256]{2,1,0:T(8,128)(2,1)S(1)} all-to-all(bf16[8,96,256]{2,1,0:T(8,128)(2,1)S(1)} %bitcast.19), channel_id=1, replica_groups={{0,1,2,3,4,5,6,7},{8,9,10,11,12,13,14,15},{16,17,18,19,20,21,22,23},{24..., dimensions={0} | all-to-all | bytes 786432 | tf_op jit(solution)/shard_map/all_to_all | solution.py:368
  76.5 0.1 reduce_sum.12
  76.6 2.7 %collective-permute-start.3 = (bf16[96,256]{1,0:T(8,128)(2,1)S(1)}, bf16[96,256]{1,0:T(8,128)(2,1)S(1)}, u32[]{:S(2)}, u32[]{:S(2)}) collective-permute-start(bf16[96,256]{1,0:T(8,128)(2,1)S(1)} %reduce_sum.12), channel_id=1, source_target_pairs={{0,8},{1,9},{2,10},{3,11},{4,12},{5,13},{6,14},{7,15},{8,0},{9,1},... | collective-permute-start | bytes 147464 | tf_op jit(solution)/shard_map/ppermute | solution.py:371
  79.2 2.9 %collective-permute-done.3 = bf16[96,256]{1,0:T(8,128)(2,1)S(1)} collective-permute-done((bf16[96,256]{1,0:T(8,128)(2,1)S(1)}, bf16[96,256]{1,0:T(8,128)(2,1)S(1)}, u32[]{:S(2)}, u32[]{:S(2)}) %collective-permute-start.3) | collective-permute-done | bytes 49184 | tf_op jit(solution)/shard_map/ppermute | solution.py:371
  82.2 9.9 %all_to_all.11 = bf16[8,96,256]{2,1,0:T(8,128)(2,1)S(1)} all-to-all(bf16[8,96,256]{2,1,0:T(8,128)(2,1)S(1)} %broadcast_in_dim.18), channel_id=1, replica_groups={{0,1,2,3,4,5,6,7},{8,9,10,11,12,13,14,15},{16,17,18,19,20,21,22,23},{24..., dimensions={0} | all-to-all | bytes 786432 | tf_op jit(solution)/shard_map/all_to_all | solution.py:373
  92.1 0.0 copy-start
  92.1 0.0 collective-permute-start.4
  92.1 1.7 %collective-permute-done.4.other = bf16[768,256]{1,0:T(8,128)(2,1)S(1)} collective-permute-done((bf16[768,256]{1,0:T(8,128)(2,1)S(1)}, bf16[768,256]{1,0:T(8,128)(2,1)S(1)}, u32[]{:S(2)}, u32[]{:S(2)}) %collective-permute-start.4) | collective-permute-done | bytes 393248 | tf_op jit(solution)/shard_map/ppermute | solution.py:380
  93.8 0.0 copy-done
  93.8 2.2 %unpack.1 = (f32[256,256]{1,0:T(8,128)}, f32[4,256]{1,0:T(4,128)}, f32[1,256]{1,0:T(1,128)}, f32[1,256]{1,0:T(1,128)}, f32[256,256]{1,0:T(8,128)}, /*index=5*/f3...) custom-call(s32[1]{0:T(128)} %bitcast.refs_0_.core, bf16[768,256]{1,0:T(8,128)(2,1)} %bitcast.18, ...), custom_call_target="tpu_custom_call" | custom-call | tf_op jit(solution)/shard_map/unpack/pallas_call | solution.py:382
  (2 shorter events, 0.0 us)
Async XLA Ops:
  1.8 2.3 %collective-permute-start = (bf16[1280,256]{1,0:T(8,128)(2,1)S(1)}, bf16[1280,256]{1,0:T(8,128)(2,1)S(1)}, u32[]{:S(2)}, u32[]{:S(2)}) collective-permute-start(bf16[1280,256]{1,0:T(8,128)(2,1)S(1)} %slice.3), channel_id=1, source_target_pairs={{0,16},{16,0},{1,17},{17,1},{2,18},{18,2},{3,19},{19,3},{4,20},{20... | collective-permute-start | bytes 1966088 | tf_op jit(solution)/shard_map/ppermute | solution.py:410
  4.1 10.1 %collective-permute-start.1 = (bf16[8960,256]{1,0:T(8,128)(2,1)}, bf16[8960,256]{1,0:T(8,128)(2,1)}, u32[]{:S(2)}, u32[]{:S(2)}) collective-permute-start(bf16[8960,256]{1,0:T(8,128)(2,1)} %param.16), channel_id=1, source_target_pairs={{0,16},{16,0},{1,17},{17,1},{2,18},{18,2},{3,19},{19,3},{4,20},{20... | collective-permute-start | bytes 13762568 | tf_op jit(solution)/shard_map/ppermute | solution.py:414
  60.3 1.7 %collective-permute-start.2 = (bf16[768,256]{1,0:T(8,128)(2,1)S(1)}, bf16[768,256]{1,0:T(8,128)(2,1)S(1)}, u32[]{:S(2)}, u32[]{:S(2)}) collective-permute-start(bf16[768,256]{1,0:T(8,128)(2,1)S(1)} %get-tuple-element.34), channel_id=1, source_target_pairs={{0,16},{16,0},{1,17},{17,1},{2,18},{18,2},{3,19},{19,3},{4,20},{20... | collective-permute-start | bytes 1179656 | tf_op jit(solution)/shard_map/ppermute | solution.py:378
  76.6 5.6 %collective-permute-start.3 = (bf16[96,256]{1,0:T(8,128)(2,1)S(1)}, bf16[96,256]{1,0:T(8,128)(2,1)S(1)}, u32[]{:S(2)}, u32[]{:S(2)}) collective-permute-start(bf16[96,256]{1,0:T(8,128)(2,1)S(1)} %reduce_sum.12), channel_id=1, source_target_pairs={{0,8},{1,9},{2,10},{3,11},{4,12},{5,13},{6,14},{7,15},{8,0},{9,1},... | collective-permute-start | bytes 147464 | tf_op jit(solution)/shard_map/ppermute | solution.py:371
  92.1 1.7 %copy-start = (bf16[8,96,256]{2,1,0:T(8,128)(2,1)}, bf16[8,96,256]{2,1,0:T(8,128)(2,1)S(1)}, u32[]{:S(2)}) copy-start(bf16[8,96,256]{2,1,0:T(8,128)(2,1)S(1)} %all_to_all.11) | copy-start | bytes 1179652
  92.1 1.7 %collective-permute-start.4 = (bf16[768,256]{1,0:T(8,128)(2,1)S(1)}, bf16[768,256]{1,0:T(8,128)(2,1)S(1)}, u32[]{:S(2)}, u32[]{:S(2)}) collective-permute-start(bf16[768,256]{1,0:T(8,128)(2,1)S(1)} %bitcast.17), channel_id=1, source_target_pairs={{0,16},{16,0},{1,17},{17,1},{2,18},{18,2},{3,19},{19,3},{4,20},{20... | collective-permute-start | bytes 1179656 | tf_op jit(solution)/shard_map/ppermute | solution.py:380

commit v6 on v5

--- a/solution.py
+++ b/solution.py
@@ -19,9 +19,9 @@
 ROWS = 1280
 SUB = 640
 ORDER = (
-    "Atl", "Apre", "Aln1", "Aln2", "Ahid", "Atsm", "Abranch", "Alnh", "Bpre", "Bln1", "Alg",
-    "Btl", "Alsm", "facts", "Bln2", "Agh", "Ahs", "Bhid", "Albh", "Btsm", "Bbranch", "Azed",
-    "Atwo", "Blnh", "Ainn", "Aone", "Albb", "Blg", "Albf", "Alat", "Alats", "Blsm", "Bgh",
+    "Atl", "Apre", "Aln1", "Atsm", "Aln2", "Btl", "Ahid", "Abranch", "Bpre", "Alnh", "Bln1",
+    "Alg", "Bln2", "Alsm", "facts", "Agh", "Ahs", "Btsm", "Albh", "Bhid", "Bbranch", "Azed",
+    "Atwo", "Ainn", "Blnh", "Blg", "Aone", "Albb", "Albf", "Blsm", "Alat", "Alats", "Bgh",
     "Bhs", "Blbh", "Bzed", "Btwo", "Binn", "Bone", "Blbb", "Blbf", "Blat", "Blats",
 )
 F32 = jnp.float32
@@ -84,34 +84,16 @@
 
 def tower(scale, first, first_block, last_block, *refs):
     (core, latent_ref, moved_ref, action_ref, code_ref, length_ref) = refs[:6]
-    (w_lat, w_act, gain_in, gain_bl, gain_he, w_one, w_two, w_chance, w_value, w_target) = refs[6:16]
+    (w_lat, gain_in, gain_bl, gain_he, w_one, w_two, heads, encoder, acts, picks, spread) = refs[6:17]
     if first:
-        grad_latent, head_sums, sums, heads, encoder, acts, picks, spread = refs[16:24]
-        act_hots, facts_kept = refs[24:]
+        grad_latent, head_sums, sums, act_hots, facts_kept = refs[17:]
     else:
-        head_before, before, _, grad_latent, stay, send = refs[16:22]
-        heads, encoder, acts, picks, spread, act_hots, facts_kept, head_sums, sums, packed = refs[22:]
+        head_before, before, _, grad_latent, stay, send = refs[17:23]
+        act_hots, facts_kept, head_sums, sums, packed = refs[23:]
     rows = latent_ref.shape[0]
 
     @pl.when(pl.program_id(0) == 0)
     def _():
-        gap = jnp.zeros((CODE_AT - BINS, D), F32)
-        heads[...] = jnp.concatenate(
-            [w_value[...].astype(F32), gap, w_chance[...].astype(F32)], axis=0
-        ).astype(BF16)
-        encoder[...] = jnp.concatenate(
-            [w_target[...].astype(F32), jnp.zeros((WIDE - BINS, D), F32)], axis=0
-        ).astype(BF16)
-        acts[...] = jnp.concatenate(
-            [w_act[...].astype(F32), jnp.zeros((16 - ACTIONS, D), F32)], axis=0
-        ).astype(BF16)
-        row = lax.broadcasted_iota(jnp.int32, (48, D), 0)
-        col = lax.broadcasted_iota(jnp.int32, (48, D), 1)
-        coded = (row < CODES) & (col == row + 128 - CODES)
-        picks[...] = jnp.where(coded | ((row == CODES) & (col >= 128)), 1.0, 0.0).astype(BF16)
-        row = UNROLL * lax.broadcasted_iota(jnp.int32, (128, SUB), 0)
-        col = lax.broadcasted_iota(jnp.int32, (128, SUB), 1)
-        spread[...] = jnp.where((col >= row) & (col < row + UNROLL), 1.0, 0.0).astype(BF16)
         head_sums[...] = jnp.zeros_like(head_sums) if first else head_before[...]
         sums[...] = jnp.zeros_like(sums) if first else before[...]
 
@@ -293,6 +275,35 @@
     gain_he[...] = packed[AT_GAIN + 2 : AT_GAIN + 3, :]
 
 
+def prepare(w_act, w_chance, w_value, w_target, heads, encoder, acts, picks, spread):
+    gap = jnp.zeros((CODE_AT - BINS, D), F32)
+    heads[...] = jnp.concatenate(
+        [w_value[...].astype(F32), gap, w_chance[...].astype(F32)], axis=0
+    ).astype(BF16)
+    encoder[...] = jnp.concatenate(
+        [w_target[...].astype(F32), jnp.zeros((WIDE - BINS, D), F32)], axis=0
+    ).astype(BF16)
+    acts[...] = jnp.concatenate(
+        [w_act[...].astype(F32), jnp.zeros((16 - ACTIONS, D), F32)], axis=0
+    ).astype(BF16)
+    row = lax.broadcasted_iota(jnp.int32, (48, D), 0)
+    col = lax.broadcasted_iota(jnp.int32, (48, D), 1)
+    coded = (row < CODES) & (col == row + 128 - CODES)
+    picks[...] = jnp.where(coded | ((row == CODES) & (col >= 128)), 1.0, 0.0).astype(BF16)
+    row = UNROLL * lax.broadcasted_iota(jnp.int32, (128, SUB), 0)
+    col = lax.broadcasted_iota(jnp.int32, (128, SUB), 1)
+    spread[...] = jnp.where((col >= row) & (col < row + UNROLL), 1.0, 0.0).astype(BF16)
+
+
+def prepare_weights(*weights):
+    shapes = ((WIDE, D), (WIDE, D), (16, D), (48, D), (128, SUB))
+    return pl.pallas_call(
+        prepare,
+        out_shape=[jax.ShapeDtypeStruct(s, BF16) for s in shapes],
+        name="prepare",
+    )(*weights)
+
+
 def run_tower(scale, core, at, steps, latent, moved, index, weights, before):
     rows = latent.shape[0]
 
@@ -315,11 +326,6 @@
     in_specs += [whole(w) for w in weights]
     args = [core, latent, moved, *index, *weights]
     scratch = [
-        pltpu.VMEM((WIDE, D), BF16),
-        pltpu.VMEM((WIDE, D), BF16),
-        pltpu.VMEM((16, D), BF16),
-        pltpu.VMEM((48, D), BF16),
-        pltpu.VMEM((128, SUB), BF16),
         pltpu.VMEM((2, 16, ROWS), BF16),
         pltpu.VMEM((2, 48, ROWS), BF16),
     ]
@@ -378,6 +384,7 @@
     mine = (stay + lax.ppermute(send, "grp", swap).astype(F32)).astype(BF16)
     mine = sum_over_chips(mine)
     other = pltpu.with_memory_space_constraint(lax.ppermute(mine, "grp", swap), pltpu.VMEM)
+    mine = pltpu.with_memory_space_constraint(mine, pltpu.VMEM)
     sizes = (D, ACTIONS, 1, 1, D, D, 1, CODES, BINS)
     return pl.pallas_call(
         unpack,
@@ -410,20 +417,10 @@
     moved_a = lax.ppermute(future_latent[:ROWS], "grp", swap)
     traj_total = lengths.shape[0] * lax.axis_size("grp") * lax.axis_size("batch")
     index = (actions.reshape(-1, 128), codes.reshape(-1, 128), lengths.reshape(-1, SUB // UNROLL))
-    moved_a, future_latent = lax.optimization_barrier((moved_a, future_latent))
+    ready = prepare_weights(w_act, w_chance.T, w_value.T, w_target.T)
+    moved_a, ready, future_latent = lax.optimization_barrier((moved_a, ready, future_latent))
+    weights = (w_lat, gain_input[None], gain_block[None], gain_head[None], w_one, w_two, *ready)
     moved_b = lax.ppermute(future_latent, "grp", swap)
-    weights = (
-        w_lat,
-        w_act,
-        gain_input[None],
-        gain_block[None],
-        gain_head[None],
-        w_one,
-        w_two,
-        w_chance.T,
-        w_value.T,
-        w_target.T,
-    )
     scale = 1.0 / math.sqrt(traj_total)
     core = lax.axis_index("grp").astype(jnp.int32).reshape(1)
     part = run_tower(scale, core, 0, 1, latent, moved_a, index, weights, None)

time: 96.4 us -> 94.1 us (0.976)
  waiting for transfers between devices: 7.95 us -> 6.01 us
    pallas_call x0 -> x1, Pallas kernels: none -> 2.01 us  [prepare_weights(): pl.pallas_call(prepare, out_shape=[jax.ShapeDtypeStruct(s, BF16) for s in...]
    ppermute x1, waiting for transfers between devices: 1.72 us -> 0.01 us  [body(): moved_a = lax.ppermute(future_latent[:ROWS], 'grp', swap)]
    pallas_call x2, Pallas kernels: 55.9 us -> 54.6 us  [run_tower(): pl.pallas_call(functools.partial(tower, scale, first, at, at + steps - 1)...]
    pallas_call x1, Pallas kernels: 2.22 us -> 1.22 us  [finish(): pl.pallas_call(unpack, in_specs=[pl.BlockSpec(memory_space=pltpu.SMEM)] +...]
  transfers between devices with their start and end apart: 5 -> 5, of which waited for: 4 -> 3; matrix products, arithmetic and copies ran while one was open for 0% -> 0% of each run, Pallas kernels for 10% -> 12%
where the time goes in v6:
time: 94.1 us; the launch traced here: 93.8 us
  Pallas kernels  57.8 us (61%)
  blocking collectives  24.3 us (26%)
  waiting for transfers between devices  6.01 us (6%)
  starting transfers between devices  3.73 us (4%)
  local copies, waits for them, and re-layouts  1.16 us (1%)
    pallas_call x2, Pallas kernels, run_tower(): pl.pallas_call(functools.partial(tower, scale, first, at, at + steps - 1)...  54.6 us
    all_to_all x1, blocking collectives, sum_over_chips(): share = swap(mine.reshape(near, -1, D))  14.4 us
    all_to_all x1, blocking collectives, sum_over_chips(): swap(jnp.broadcast_to(share[None], (near, *share.shape))).reshape(rows, D)  9.89 us
    ppermute x1, waiting for transfers between devices, sum_over_chips(): lax.ppermute(share, 'batch', [(i, (i + near) % count) for i in range(coun...  2.93 us
    ppermute x1, starting transfers between devices, sum_over_chips(): lax.ppermute(share, 'batch', [(i, (i + near) % count) for i in range(coun...  2.65 us
    pallas_call x1, Pallas kernels, prepare_weights(): pl.pallas_call(prepare, out_shape=[jax.ShapeDtypeStruct(s, BF16) for s in...  2.01 us
  transfers between devices with their start and end apart: 5, of which 3 were waited for; matrix products, arithmetic and copies ran while one was open for 0% of the time, Pallas kernels for 12%

profile of v6, /device:TPU:0, one launch (start us, length us, event | category | flops | bytes accessed | tf_op | source)
XLA Modules:
  0.0 93.8 jit_solution(5560338242926389844)
XLA Ops:
  0.6 1.1 %slice.3 = bf16[1280,256]{1,0:T(8,128)(2,1)S(1)} slice(bf16[8960,256]{1,0:T(8,128)(2,1)} %param.16), slice={[0:1280], [0:256]} | slice | bytes 1310720 | tf_op jit(solution)/shard_map/slice | solution.py:417
  1.8 0.6 collective-permute-start
  2.3 2.0 %prepare.1 = (bf16[640,256]{1,0:T(8,128)(2,1)}, bf16[640,256]{1,0:T(8,128)(2,1)}, bf16[16,256]{1,0:T(8,128)(2,1)}, bf16[48,256]{1,0:T(8,128)(2,1)}, bf16[128,640]{1,0:T(8,128)(2,1)}) custom-call(bf16[4,256]{1,0:T(4,128)(2,1)} %w_act.1, bf16[32,256]{1,0:T(8,128)(2,1)} %bitcast.22, bf16[601,256]{1,0:T(8,128)(2,1)} %bitcast.20, bf16[601,256]{1,0:T(8,128)(2,1)} %bitcast.21), custom_call_target="tpu_custom_call" | custom-call | tf_op jit(solution)/shard_map/prepare/pallas_call | solution.py:300
  4.3 0.0 collective-permute-done.refs_2_
  4.3 0.1 collective-permute-start.1
  4.4 9.5 %tower.2 = (f32[8960,256]{1,0:T(8,128)}, f32[256,640]{1,0:T(8,128)S(1)}, f32[808,256]{1,0:T(8,128)S(1)}) custom-call(s32[1]{0:T(128)} %bitcast.refs_0_.core, bf16[8960,256]{1,0:T(8,128)(2,1)} %refs_1_.3, bf16[1280,256]{1,0:T(8,128)(2,1)S(1)} %collective-permute-done.refs_2_, s32[70,128]{1,0:T(8,128)} %bitcast.24, s32[70,128]{1,0:T(8,128)} %bitcast.26, ...), custom_call_target="tpu_custom_call" | custom-call | flops 3200000000 | bytes 2621440 | tf_op jit(solution)/shard_map/tower/pallas_call | solution.py:343
  14.0 0.0 collective-permute-done.1.refs_2_
  14.0 45.1 %tower.3 = (f32[8960,256]{1,0:T(8,128)}, f32[768,256]{1,0:T(8,128)S(1)}, bf16[768,256]{1,0:T(8,128)(2,1)S(1)}) custom-call(s32[1]{0:T(128)} %bitcast.refs_0_.core, bf16[8960,256]{1,0:T(8,128)(2,1)} %refs_1_.3, bf16[8960,256]{1,0:T(8,128)(2,1)} %collective-permute-done.1.refs_2_, s32[70,128]{1,0:T(8,128)} %bitcast.25, ...), custom_call_target="tpu_custom_call", output_to_operand_aliasing={{0}: (19, {})} | custom-call | flops 19200000000 | bytes 15728640 | tf_op jit(solution)/shard_map/tower/pallas_call | solution.py:343
  59.0 0.4 collective-permute-start.2
  59.5 1.3 %collective-permute-done.2 = bf16[768,256]{1,0:T(8,128)(2,1)S(1)} collective-permute-done((bf16[768,256]{1,0:T(8,128)(2,1)S(1)}, bf16[768,256]{1,0:T(8,128)(2,1)S(1)}, u32[]{:S(2)}, u32[]{:S(2)}) %collective-permute-start.2) | collective-permute-done | bytes 393248 | tf_op jit(solution)/shard_map/ppermute | solution.py:384
  60.8 0.1 add_convert_fusion
  60.9 14.4 %all_to_all.10 = bf16[8,96,256]{2,1,0:T(8,128)(2,1)S(1)} all-to-all(bf16[8,96,256]{2,1,0:T(8,128)(2,1)S(1)} %bitcast.19), channel_id=1, replica_groups={{0,1,2,3,4,5,6,7},{8,9,10,11,12,13,14,15},{16,17,18,19,20,21,22,23},{24..., dimensions={0} | all-to-all | bytes 786432 | tf_op jit(solution)/shard_map/all_to_all | solution.py:374
  75.3 0.1 reduce_sum.12
  75.4 2.6 %collective-permute-start.3 = (bf16[96,256]{1,0:T(8,128)(2,1)S(1)}, bf16[96,256]{1,0:T(8,128)(2,1)S(1)}, u32[]{:S(2)}, u32[]{:S(2)}) collective-permute-start(bf16[96,256]{1,0:T(8,128)(2,1)S(1)} %reduce_sum.12), channel_id=1, source_target_pairs={{0,8},{1,9},{2,10},{3,11},{4,12},{5,13},{6,14},{7,15},{8,0},{9,1},... | collective-permute-start | bytes 147464 | tf_op jit(solution)/shard_map/ppermute | solution.py:377
  78.0 2.9 %collective-permute-done.3 = bf16[96,256]{1,0:T(8,128)(2,1)S(1)} collective-permute-done((bf16[96,256]{1,0:T(8,128)(2,1)S(1)}, bf16[96,256]{1,0:T(8,128)(2,1)S(1)}, u32[]{:S(2)}, u32[]{:S(2)}) %collective-permute-start.3) | collective-permute-done | bytes 49184 | tf_op jit(solution)/shard_map/ppermute | solution.py:377
  81.0 9.9 %all_to_all.11 = bf16[8,96,256]{2,1,0:T(8,128)(2,1)S(1)} all-to-all(bf16[8,96,256]{2,1,0:T(8,128)(2,1)S(1)} %broadcast_in_dim.18), channel_id=1, replica_groups={{0,1,2,3,4,5,6,7},{8,9,10,11,12,13,14,15},{16,17,18,19,20,21,22,23},{24..., dimensions={0} | all-to-all | bytes 786432 | tf_op jit(solution)/shard_map/all_to_all | solution.py:379
  90.9 0.0 collective-permute-start.4
  90.9 1.7 %collective-permute-done.4.other = bf16[768,256]{1,0:T(8,128)(2,1)S(1)} collective-permute-done((bf16[768,256]{1,0:T(8,128)(2,1)S(1)}, bf16[768,256]{1,0:T(8,128)(2,1)S(1)}, u32[]{:S(2)}, u32[]{:S(2)}) %collective-permute-start.4) | collective-permute-done | bytes 393248 | tf_op jit(solution)/shard_map/ppermute | solution.py:386
  92.6 1.2 %unpack.1 = (f32[256,256]{1,0:T(8,128)}, f32[4,256]{1,0:T(4,128)}, f32[1,256]{1,0:T(1,128)}, f32[1,256]{1,0:T(1,128)}, f32[256,256]{1,0:T(8,128)}, /*index=5*/f3...) custom-call(s32[1]{0:T(128)} %bitcast.refs_0_.core, bf16[768,256]{1,0:T(8,128)(2,1)S(1)} %bitcast.18, ...), custom_call_target="tpu_custom_call" | custom-call | tf_op jit(solution)/shard_map/unpack/pallas_call | solution.py:389
  (2 shorter events, 0.0 us)
Async XLA Ops:
  1.8 2.6 %collective-permute-start = (bf16[1280,256]{1,0:T(8,128)(2,1)S(1)}, bf16[1280,256]{1,0:T(8,128)(2,1)S(1)}, u32[]{:S(2)}, u32[]{:S(2)}) collective-permute-start(bf16[1280,256]{1,0:T(8,128)(2,1)S(1)} %slice.3), channel_id=1, source_target_pairs={{0,16},{16,0},{1,17},{17,1},{2,18},{18,2},{3,19},{19,3},{4,20},{20... | collective-permute-start | bytes 1966088 | tf_op jit(solution)/shard_map/ppermute | solution.py:417
  4.3 9.6 %collective-permute-start.1 = (bf16[8960,256]{1,0:T(8,128)(2,1)}, bf16[8960,256]{1,0:T(8,128)(2,1)}, u32[]{:S(2)}, u32[]{:S(2)}) collective-permute-start(bf16[8960,256]{1,0:T(8,128)(2,1)} %param.16), channel_id=1, source_target_pairs={{0,16},{16,0},{1,17},{17,1},{2,18},{18,2},{3,19},{19,3},{4,20},{20... | collective-permute-start | bytes 13762568 | tf_op jit(solution)/shard_map/ppermute | solution.py:423
  59.0 1.8 %collective-permute-start.2 = (bf16[768,256]{1,0:T(8,128)(2,1)S(1)}, bf16[768,256]{1,0:T(8,128)(2,1)S(1)}, u32[]{:S(2)}, u32[]{:S(2)}) collective-permute-start(bf16[768,256]{1,0:T(8,128)(2,1)S(1)} %get-tuple-element.54), channel_id=1, source_target_pairs={{0,16},{16,0},{1,17},{17,1},{2,18},{18,2},{3,19},{19,3},{4,20},{20... | collective-permute-start | bytes 1179656 | tf_op jit(solution)/shard_map/ppermute | solution.py:384
  75.4 5.6 %collective-permute-start.3 = (bf16[96,256]{1,0:T(8,128)(2,1)S(1)}, bf16[96,256]{1,0:T(8,128)(2,1)S(1)}, u32[]{:S(2)}, u32[]{:S(2)}) collective-permute-start(bf16[96,256]{1,0:T(8,128)(2,1)S(1)} %reduce_sum.12), channel_id=1, source_target_pairs={{0,8},{1,9},{2,10},{3,11},{4,12},{5,13},{6,14},{7,15},{8,0},{9,1},... | collective-permute-start | bytes 147464 | tf_op jit(solution)/shard_map/ppermute | solution.py:377
  90.9 1.7 %collective-permute-start.4 = (bf16[768,256]{1,0:T(8,128)(2,1)S(1)}, bf16[768,256]{1,0:T(8,128)(2,1)S(1)}, u32[]{:S(2)}, u32[]{:S(2)}) collective-permute-start(bf16[768,256]{1,0:T(8,128)(2,1)S(1)} %bitcast.17), channel_id=1, source_target_pairs={{0,16},{16,0},{1,17},{17,1},{2,18},{18,2},{3,19},{19,3},{4,20},{20... | collective-permute-start | bytes 1179656 | tf_op jit(solution)/shard_map/ppermute | solution.py:386

commit v7 on v6

--- a/solution.py
+++ b/solution.py
@@ -19,9 +19,9 @@
 ROWS = 1280
 SUB = 640
 ORDER = (
-    "Atl", "Apre", "Aln1", "Atsm", "Aln2", "Btl", "Ahid", "Abranch", "Bpre", "Alnh", "Bln1",
-    "Alg", "Bln2", "Alsm", "facts", "Agh", "Ahs", "Btsm", "Albh", "Bhid", "Bbranch", "Azed",
-    "Atwo", "Ainn", "Blnh", "Blg", "Aone", "Albb", "Albf", "Blsm", "Alat", "Alats", "Bgh",
+    "Apre", "Atl", "Bpre", "Aln1", "Aln2", "Atsm", "Ahid", "Abranch", "Btl", "Alnh", "Alg",
+    "Bln1", "Bln2", "Alsm", "facts", "Agh", "Ahs", "Bhid", "Albh", "Bbranch", "Azed", "Atwo",
+    "Blnh", "Ainn", "Aone", "Blg", "Btsm", "Blsm", "Albb", "Albf", "Alat", "Alats", "Bgh",
     "Bhs", "Blbh", "Bzed", "Btwo", "Binn", "Bone", "Blbb", "Blbf", "Blat", "Blats",
 )
 F32 = jnp.float32

time: 94.1 us -> 93.6 us (level)
  transfers between devices with their start and end apart: 5 -> 5, of which waited for: 3 -> 3; matrix products, arithmetic and copies ran while one was open for 0% -> 0% of each run, Pallas kernels for 12% -> 13%
where the time goes in v7:
time: 93.6 us; the launch traced here: 93.3 us
  Pallas kernels  57.3 us (61%)
  blocking collectives  24.3 us (26%)
  waiting for transfers between devices  6 us (6%)
  starting transfers between devices  3.74 us (4%)
  local copies, waits for them, and re-layouts  1.16 us (1%)
    pallas_call x2, Pallas kernels, run_tower(): pl.pallas_call(functools.partial(tower, scale, first, at, at + steps - 1)...  54.1 us
    all_to_all x1, blocking collectives, sum_over_chips(): share = swap(mine.reshape(near, -1, D))  14.4 us
    all_to_all x1, blocking collectives, sum_over_chips(): swap(jnp.broadcast_to(share[None], (near, *share.shape))).reshape(rows, D)  9.89 us
    ppermute x1, waiting for transfers between devices, sum_over_chips(): lax.ppermute(share, 'batch', [(i, (i + near) % count) for i in range(coun...  2.92 us
    ppermute x1, starting transfers between devices, sum_over_chips(): lax.ppermute(share, 'batch', [(i, (i + near) % count) for i in range(coun...  2.66 us
    pallas_call x1, Pallas kernels, prepare_weights(): pl.pallas_call(prepare, out_shape=[jax.ShapeDtypeStruct(s, BF16) for s in...  2.01 us
  transfers between devices with their start and end apart: 5, of which 3 were waited for; matrix products, arithmetic and copies ran while one was open for 0% of the time, Pallas kernels for 13%

profile of v7, /device:TPU:0, one launch (start us, length us, event | category | flops | bytes accessed | tf_op | source)
XLA Modules:
  0.0 93.3 jit_solution(5826872673654903213)
XLA Ops:
  0.6 1.1 %slice.3 = bf16[1280,256]{1,0:T(8,128)(2,1)S(1)} slice(bf16[8960,256]{1,0:T(8,128)(2,1)} %param.16), slice={[0:1280], [0:256]} | slice | bytes 1310720 | tf_op jit(solution)/shard_map/slice | solution.py:417
  1.8 0.6 collective-permute-start
  2.3 2.0 %prepare.1 = (bf16[640,256]{1,0:T(8,128)(2,1)}, bf16[640,256]{1,0:T(8,128)(2,1)}, bf16[16,256]{1,0:T(8,128)(2,1)}, bf16[48,256]{1,0:T(8,128)(2,1)}, bf16[128,640]{1,0:T(8,128)(2,1)}) custom-call(bf16[4,256]{1,0:T(4,128)(2,1)} %w_act.1, bf16[32,256]{1,0:T(8,128)(2,1)} %bitcast.22, bf16[601,256]{1,0:T(8,128)(2,1)} %bitcast.20, bf16[601,256]{1,0:T(8,128)(2,1)} %bitcast.21), custom_call_target="tpu_custom_call" | custom-call | tf_op jit(solution)/shard_map/prepare/pallas_call | solution.py:300
  4.3 0.0 collective-permute-done.refs_2_
  4.3 0.1 collective-permute-start.1
  4.4 9.8 %tower.2 = (f32[8960,256]{1,0:T(8,128)}, f32[256,640]{1,0:T(8,128)S(1)}, f32[808,256]{1,0:T(8,128)S(1)}) custom-call(s32[1]{0:T(128)} %bitcast.refs_0_.core, bf16[8960,256]{1,0:T(8,128)(2,1)} %refs_1_.3, bf16[1280,256]{1,0:T(8,128)(2,1)S(1)} %collective-permute-done.refs_2_, s32[70,128]{1,0:T(8,128)} %bitcast.24, s32[70,128]{1,0:T(8,128)} %bitcast.26, ...), custom_call_target="tpu_custom_call" | custom-call | flops 3200000000 | bytes 2621440 | tf_op jit(solution)/shard_map/tower/pallas_call | solution.py:343
  14.2 0.0 collective-permute-done.1.refs_2_
  14.2 44.3 %tower.3 = (f32[8960,256]{1,0:T(8,128)}, f32[768,256]{1,0:T(8,128)S(1)}, bf16[768,256]{1,0:T(8,128)(2,1)S(1)}) custom-call(s32[1]{0:T(128)} %bitcast.refs_0_.core, bf16[8960,256]{1,0:T(8,128)(2,1)} %refs_1_.3, bf16[8960,256]{1,0:T(8,128)(2,1)} %collective-permute-done.1.refs_2_, s32[70,128]{1,0:T(8,128)} %bitcast.25, ...), custom_call_target="tpu_custom_call", output_to_operand_aliasing={{0}: (19, {})} | custom-call | flops 19200000000 | bytes 15728640 | tf_op jit(solution)/shard_map/tower/pallas_call | solution.py:343
  58.5 0.4 collective-permute-start.2
  59.0 1.3 %collective-permute-done.2 = bf16[768,256]{1,0:T(8,128)(2,1)S(1)} collective-permute-done((bf16[768,256]{1,0:T(8,128)(2,1)S(1)}, bf16[768,256]{1,0:T(8,128)(2,1)S(1)}, u32[]{:S(2)}, u32[]{:S(2)}) %collective-permute-start.2) | collective-permute-done | bytes 393248 | tf_op jit(solution)/shard_map/ppermute | solution.py:384
  60.3 0.1 add_convert_fusion
  60.4 14.4 %all_to_all.10 = bf16[8,96,256]{2,1,0:T(8,128)(2,1)S(1)} all-to-all(bf16[8,96,256]{2,1,0:T(8,128)(2,1)S(1)} %bitcast.19), channel_id=1, replica_groups={{0,1,2,3,4,5,6,7},{8,9,10,11,12,13,14,15},{16,17,18,19,20,21,22,23},{24..., dimensions={0} | all-to-all | bytes 786432 | tf_op jit(solution)/shard_map/all_to_all | solution.py:374
  74.8 0.1 reduce_sum.12
  74.8 2.7 %collective-permute-start.3 = (bf16[96,256]{1,0:T(8,128)(2,1)S(1)}, bf16[96,256]{1,0:T(8,128)(2,1)S(1)}, u32[]{:S(2)}, u32[]{:S(2)}) collective-permute-start(bf16[96,256]{1,0:T(8,128)(2,1)S(1)} %reduce_sum.12), channel_id=1, source_target_pairs={{0,8},{1,9},{2,10},{3,11},{4,12},{5,13},{6,14},{7,15},{8,0},{9,1},... | collective-permute-start | bytes 147464 | tf_op jit(solution)/shard_map/ppermute | solution.py:377
  77.5 2.9 %collective-permute-done.3 = bf16[96,256]{1,0:T(8,128)(2,1)S(1)} collective-permute-done((bf16[96,256]{1,0:T(8,128)(2,1)S(1)}, bf16[96,256]{1,0:T(8,128)(2,1)S(1)}, u32[]{:S(2)}, u32[]{:S(2)}) %collective-permute-start.3) | collective-permute-done | bytes 49184 | tf_op jit(solution)/shard_map/ppermute | solution.py:377
  80.5 9.9 %all_to_all.11 = bf16[8,96,256]{2,1,0:T(8,128)(2,1)S(1)} all-to-all(bf16[8,96,256]{2,1,0:T(8,128)(2,1)S(1)} %broadcast_in_dim.18), channel_id=1, replica_groups={{0,1,2,3,4,5,6,7},{8,9,10,11,12,13,14,15},{16,17,18,19,20,21,22,23},{24..., dimensions={0} | all-to-all | bytes 786432 | tf_op jit(solution)/shard_map/all_to_all | solution.py:379
  90.4 0.0 collective-permute-start.4
  90.4 1.7 %collective-permute-done.4.other = bf16[768,256]{1,0:T(8,128)(2,1)S(1)} collective-permute-done((bf16[768,256]{1,0:T(8,128)(2,1)S(1)}, bf16[768,256]{1,0:T(8,128)(2,1)S(1)}, u32[]{:S(2)}, u32[]{:S(2)}) %collective-permute-start.4) | collective-permute-done | bytes 393248 | tf_op jit(solution)/shard_map/ppermute | solution.py:386
  92.1 1.2 %unpack.1 = (f32[256,256]{1,0:T(8,128)}, f32[4,256]{1,0:T(4,128)}, f32[1,256]{1,0:T(1,128)}, f32[1,256]{1,0:T(1,128)}, f32[256,256]{1,0:T(8,128)}, /*index=5*/f3...) custom-call(s32[1]{0:T(128)} %bitcast.refs_0_.core, bf16[768,256]{1,0:T(8,128)(2,1)S(1)} %bitcast.18, ...), custom_call_target="tpu_custom_call" | custom-call | tf_op jit(solution)/shard_map/unpack/pallas_call | solution.py:389
  (2 shorter events, 0.0 us)
Async XLA Ops:
  1.8 2.6 %collective-permute-start = (bf16[1280,256]{1,0:T(8,128)(2,1)S(1)}, bf16[1280,256]{1,0:T(8,128)(2,1)S(1)}, u32[]{:S(2)}, u32[]{:S(2)}) collective-permute-start(bf16[1280,256]{1,0:T(8,128)(2,1)S(1)} %slice.3), channel_id=1, source_target_pairs={{0,16},{16,0},{1,17},{17,1},{2,18},{18,2},{3,19},{19,3},{4,20},{20... | collective-permute-start | bytes 1966088 | tf_op jit(solution)/shard_map/ppermute | solution.py:417
  4.3 9.9 %collective-permute-start.1 = (bf16[8960,256]{1,0:T(8,128)(2,1)}, bf16[8960,256]{1,0:T(8,128)(2,1)}, u32[]{:S(2)}, u32[]{:S(2)}) collective-permute-start(bf16[8960,256]{1,0:T(8,128)(2,1)} %param.16), channel_id=1, source_target_pairs={{0,16},{16,0},{1,17},{17,1},{2,18},{18,2},{3,19},{19,3},{4,20},{20... | collective-permute-start | bytes 13762568 | tf_op jit(solution)/shard_map/ppermute | solution.py:423
  58.5 1.8 %collective-permute-start.2 = (bf16[768,256]{1,0:T(8,128)(2,1)S(1)}, bf16[768,256]{1,0:T(8,128)(2,1)S(1)}, u32[]{:S(2)}, u32[]{:S(2)}) collective-permute-start(bf16[768,256]{1,0:T(8,128)(2,1)S(1)} %get-tuple-element.54), channel_id=1, source_target_pairs={{0,16},{16,0},{1,17},{17,1},{2,18},{18,2},{3,19},{19,3},{4,20},{20... | collective-permute-start | bytes 1179656 | tf_op jit(solution)/shard_map/ppermute | solution.py:384
  74.8 5.6 %collective-permute-start.3 = (bf16[96,256]{1,0:T(8,128)(2,1)S(1)}, bf16[96,256]{1,0:T(8,128)(2,1)S(1)}, u32[]{:S(2)}, u32[]{:S(2)}) collective-permute-start(bf16[96,256]{1,0:T(8,128)(2,1)S(1)} %reduce_sum.12), channel_id=1, source_target_pairs={{0,8},{1,9},{2,10},{3,11},{4,12},{5,13},{6,14},{7,15},{8,0},{9,1},... | collective-permute-start | bytes 147464 | tf_op jit(solution)/shard_map/ppermute | solution.py:377
  90.4 1.7 %collective-permute-start.4 = (bf16[768,256]{1,0:T(8,128)(2,1)S(1)}, bf16[768,256]{1,0:T(8,128)(2,1)S(1)}, u32[]{:S(2)}, u32[]{:S(2)}) collective-permute-start(bf16[768,256]{1,0:T(8,128)(2,1)S(1)} %bitcast.17), channel_id=1, source_target_pairs={{0,16},{16,0},{1,17},{17,1},{2,18},{18,2},{3,19},{19,3},{4,20},{20... | collective-permute-start | bytes 1179656 | tf_op jit(solution)/shard_map/ppermute | solution.py:386
